TPU v7x, 32 devices: a whole 2x2x4 slice. The times are simulated.
32 devices in a mesh: pipe: 2 (over core), node: 8 (over z, x), head: 2 (over y).
Axes of the slice: x: 2, y: 2, z: 4, core: 2. Of those that a mesh axis runs over, the one named last changes fastest.
Arguments:
- feats: bfloat16 [2, 1024, 2048], P(None, 'node', 'head'), may hold values from -20 to 20
- gain: float32 [2, 2048], P('pipe'), may hold values from 0.25 to 1.75
- w_qkv: bfloat16 [2, 3, 2048, 2048], P('pipe', None, 'node', 'head'), may hold values from -0.176776695 to 0.176776695
- w_out: bfloat16 [2, 2048, 2048], P('pipe', 'head', 'node'), may hold values from -1 to 1
- block_mask: int32 [2, 8, 8], replicated, may hold values from 0 to 1, as said below
Outputs:
- layers_out: bfloat16 [2, 2, 1024, 2048], P('pipe', None, 'node', 'head')
Inputs may be any that keep to these rules, and one draw needn't show every extreme that they name: block_mask[m, b, b] = 1; block_mask[m, b, c] is 0 unless c = b or c = b xor 2^k with k one of L - 1, L // 2 and 0, where 2^L = 8.
All inputs are finite; a program needn't handle non-finite values.
Results may differ from a plain program's by a relative error of at most 0.023.
Values may be sent and summed in bfloat16 or wider, within the bound.
A program may use at most 64 MiB of HBM per device.

v0:
```python
import jax
import jax.numpy as jnp
from jax import lax
from jax.sharding import PartitionSpec as P

HD = 128
MICRO = 2


EPS = 1e-06
NEG = -1e30


def from_partner(block, axis, apart):
    count = lax.axis_size(axis)
    route = []
    for low in range(count):
        high = low | 1 << apart
        if high != low and high < count:
            route += [(low, high), (high, low)]
    return lax.ppermute(block, axis, route)


def from_behind(value, axis, steps):
    count = lax.axis_size(axis)
    first, last = (max(0, -steps), min(count, count - steps))
    return lax.ppermute(value, axis, [(source, source + steps) for source in range(first, last)])


def partial_attend(query, key, value, keep):
    rows = query.shape[0]
    groups = query.shape[1] // HD
    q_heads = query.reshape(rows, groups, HD)
    k_heads = key.reshape(key.shape[0], groups, HD)
    v_heads = value.reshape(value.shape[0], groups, HD)
    scores = jnp.einsum("qhd,khd->hqk", q_heads, k_heads, preferred_element_type=jnp.float32) * (
        1.0 / HD**0.5
    )
    scores = jnp.where(keep[None, None, :], scores, NEG)
    top = jnp.max(scores, axis=-1)
    expo = jnp.where(keep[None, None, :], jnp.exp(scores - top[..., None]), 0.0)
    total = jnp.sum(expo, axis=-1)
    summed = jnp.einsum(
        "hqk,khd->hqd", expo.astype(jnp.bfloat16), v_heads, preferred_element_type=jnp.float32
    )
    return (summed, top, total)


def finish(summed, total):
    out = summed / total[..., None]
    rows = out.shape[1]
    return jnp.transpose(out, (1, 0, 2)).reshape(rows, -1).astype(jnp.bfloat16)


def local(feats, gain, w_qkv, w_out, block_mask):
    segment = lax.axis_index("pipe")
    me = lax.axis_index("node")
    width = lax.axis_size("node").bit_length() - 1
    bit_list = [width - 1, width // 2, 0]
    qkv_whole, out_whole = (
        lax.all_gather(w_qkv, "node", axis=2, tiled=True),
        lax.all_gather(w_out, "node", axis=2, tiled=True),
    )
    w_query = qkv_whole[0, 0]
    w_key = qkv_whole[0, 1]
    w_value = qkv_whole[0, 2]
    w_proj = out_whole[0]
    gain_row = gain[0]
    rows = feats.shape[1]
    carried = jnp.zeros_like(feats[0])
    results = []
    for tick in range(MICRO + 1):
        micro = jnp.clip(tick - segment, 0, MICRO - 1)
        fresh = feats[min(tick, MICRO - 1)]
        inputs = jnp.where(segment == 0, fresh, carried)
        whole = lax.all_gather(inputs, "head", axis=1, tiled=True)
        xf = whole.astype(jnp.float32)
        inv = lax.rsqrt(jnp.mean(xf * xf, axis=-1, keepdims=True) + EPS)
        normed = (xf * inv * gain_row).astype(jnp.bfloat16)
        query = jnp.dot(normed, w_query, preferred_element_type=jnp.float32).astype(jnp.bfloat16)
        key = jnp.dot(normed, w_key, preferred_element_type=jnp.float32).astype(jnp.bfloat16)
        value = jnp.dot(normed, w_value, preferred_element_type=jnp.float32).astype(jnp.bfloat16)
        mask_rows = lax.dynamic_index_in_dim(block_mask, micro, 0, keepdims=False)
        own_flag = mask_rows[me, me] > 0
        key_list = [key]
        value_list = [value]
        flag_list = [own_flag]
        for bit in bit_list:
            far_key, far_value = from_partner((key, value), "node", bit)
            key_list.append(far_key)
            value_list.append(far_value)
            flag_list.append(mask_rows[me, jnp.bitwise_xor(me, 1 << bit)] > 0)
        keep = jnp.repeat(jnp.stack(flag_list), rows)
        summed, top, total = partial_attend(
            query, jnp.concatenate(key_list, 0), jnp.concatenate(value_list, 0), keep
        )
        attended = finish(summed, total)
        terms = jnp.dot(attended, w_proj, preferred_element_type=jnp.float32)
        reduced = lax.psum_scatter(
            terms.astype(jnp.bfloat16), "head", scatter_dimension=1, tiled=True
        ).astype(jnp.float32)
        output = (inputs.astype(jnp.float32) + reduced).astype(jnp.bfloat16)
        results.append(output)
        if tick < MICRO:
            carried = from_behind(output, "pipe", 1)
    first = jnp.where(segment == 0, results[0], results[1])
    second = jnp.where(segment == 0, results[1], results[2])
    return jnp.stack([first, second])[None]


def solution(mesh):
    return jax.shard_map(
        local,
        mesh=mesh,
        in_specs=(
            P(None, "node", "head"),
            P("pipe", None),
            P("pipe", None, "node", "head"),
            P("pipe", "head", "node"),
            P(),
        ),
        out_specs=P("pipe", None, "node", "head"),
        check_vma=False,
    )
```

profile of v0, /device:TPU:25, one launch (start us, length us, event | category | flops | bytes accessed | tf_op | source)
XLA Modules:
  0.0 456.1 jit_solution(13671450171622768266)
XLA Ops:
  11.6 7.8 %all-gather = bf16[1,128,2048]{2,1,0:T(8,128)(2,1)S(1)} all-gather(bf16[1,128,1024]{2,1,0:T(8,128)(2,1)S(1)} %slice_select_fusion), channel_id=2, replica_groups=mesh['pipe'=2,'node'=8,'head'=2] {'head'}, dimensions={2}, use_global_device_ids=true | all-gather | bytes 786432 | tf_op jit(solution)/shard_map/all_gather | solution.py:76
  19.8 165.0 %all-gather.4.cloned.1.call-done = bf16[1,3,2048,1024]{3,2,1,0:T(8,128)(2,1)} async-done(((bf16[1,3,256,1024]{3,2,1,0:T(8,128)(2,1)}), bf16[1,3,2048,1024]{3,2,1,0:T(8,128)(2,1)}) %all-gather.4.cloned.1.call-update) | async-done | bytes 12582928 | tf_op jit(solution)/shard_map/all_gather | solution.py:61
  184.8 2.9 fusion.36
  187.8 2.9 fusion.39
  194.9 23.8 %collective-permute-done.3 = bf16[128,1024]{1,0:T(8,128)(2,1)S(1)} collective-permute-done((bf16[128,1024]{1,0:T(8,128)(2,1)S(1)}, bf16[128,1024]{1,0:T(8,128)(2,1)S(1)}, u32[]{:S(2)}, u32[]{:S(2)}) %collective-permute-start.3) | collective-permute-done | bytes 262176 | tf_op jit(solution)/shard_map/ppermute | solution.py:21
  219.0 3.7 fusion.47
  222.6 8.2 %collective-permute-done.4 = bf16[128,1024]{1,0:T(8,128)(2,1)S(1)} collective-permute-done((bf16[128,1024]{1,0:T(8,128)(2,1)S(1)}, bf16[128,1024]{1,0:T(8,128)(2,1)S(1)}, u32[]{:S(2)}, u32[]{:S(2)}) %collective-permute-start.4) | collective-permute-done | bytes 262176 | tf_op jit(solution)/shard_map/ppermute | solution.py:21
  231.9 2.8 fusion.63
  236.7 3.8 fusion.35
  240.5 40.2 %all-gather.6.cloned.1.call-done = bf16[1,1024,2048]{2,1,0:T(8,128)(2,1)} async-done(((bf16[1,1024,256]{2,1,0:T(8,128)(2,1)}), bf16[1,1024,2048]{2,1,0:T(8,128)(2,1)}) %all-gather.6.cloned.1.call-update) | async-done | bytes 4194320 | tf_op jit(solution)/shard_map/all_gather | solution.py:62
  280.7 3.7 fusion.18
  287.0 12.1 %reduce-scatter.4.cloned.1.call-done = bf16[128,1024]{1,0:T(8,128)(2,1)} async-done(((bf16[128,2048]{1,0:T(8,128)(2,1)}), bf16[128,1024]{1,0:T(8,128)(2,1)}) %reduce-scatter.4.cloned.1.call-update) | async-done | bytes 262160 | tf_op jit(solution)/shard_map/reduce_scatter | solution.py:99
  303.6 8.6 %all_gather.18 = bf16[128,2048]{1,0:T(8,128)(2,1)S(1)} all-gather(bf16[128,1024]{1,0:T(8,128)(2,1)S(1)} %bitcast_select_fusion.1), channel_id=1, replica_groups=mesh['pipe'=2,'node'=8,'head'=2] {'head'}, dimensions={1}, use_global_device_ids=true | all-gather | bytes 786432 | tf_op jit(solution)/shard_map/all_gather | solution.py:76
  312.4 3.0 fusion.37
  315.6 3.0 fusion.40
  323.5 12.3 %collective-permute-done.10 = bf16[128,1024]{1,0:T(8,128)(2,1)S(1)} collective-permute-done((bf16[128,1024]{1,0:T(8,128)(2,1)S(1)}, bf16[128,1024]{1,0:T(8,128)(2,1)S(1)}, u32[]{:S(2)}, u32[]{:S(2)}) %collective-permute-start.10) | collective-permute-done | bytes 262176 | tf_op jit(solution)/shard_map/ppermute | solution.py:21
  337.0 3.7 fusion.46
  340.6 3.2 collective-permute-done.11
  344.5 3.0 fusion.60
  349.6 3.8 fusion.34
  353.4 3.7 fusion.21
  359.7 13.8 %reduce-scatter.6.cloned.1.call-done = bf16[128,1024]{1,0:T(8,128)(2,1)} async-done(((bf16[128,2048]{1,0:T(8,128)(2,1)}), bf16[128,1024]{1,0:T(8,128)(2,1)}) %reduce-scatter.6.cloned.1.call-update) | async-done | bytes 262160 | tf_op jit(solution)/shard_map/reduce_scatter | solution.py:99
  378.1 8.4 %all_gather.19 = bf16[128,2048]{1,0:T(8,128)(2,1)S(1)} all-gather(bf16[128,1024]{1,0:T(8,128)(2,1)S(1)} %bitcast_select_fusion), channel_id=1, replica_groups=mesh['pipe'=2,'node'=8,'head'=2] {'head'}, dimensions={1}, use_global_device_ids=true | all-gather | bytes 786432 | tf_op jit(solution)/shard_map/all_gather | solution.py:76
  386.7 3.0 fusion.38
  390.0 3.0 fusion.41
  397.8 12.3 %collective-permute-done.17 = bf16[128,1024]{1,0:T(8,128)(2,1)S(1)} collective-permute-done((bf16[128,1024]{1,0:T(8,128)(2,1)S(1)}, bf16[128,1024]{1,0:T(8,128)(2,1)S(1)}, u32[]{:S(2)}, u32[]{:S(2)}) %collective-permute-start.17) | collective-permute-done | bytes 262176 | tf_op jit(solution)/shard_map/ppermute | solution.py:21
  411.3 3.7 fusion.45
  415.0 3.2 collective-permute-done.18
  418.9 2.9 fusion.57
  423.8 3.7 fusion.33
  427.5 3.7 fusion.24
  431.2 16.4 %reduce-scatter.8.cloned.1.call-done = bf16[128,1024]{1,0:T(8,128)(2,1)} async-done(((bf16[128,2048]{1,0:T(8,128)(2,1)}), bf16[128,1024]{1,0:T(8,128)(2,1)}) %reduce-scatter.8.cloned.1.call-update) | async-done | bytes 262160 | tf_op jit(solution)/shard_map/reduce_scatter | solution.py:99
  (85 shorter events, 39.4 us)
Async XLA Ops:
  6.5 1.6 copy-start.1
  6.5 5.1 %copy-start = (bf16[2,128,1024]{2,1,0:T(8,128)(2,1)S(1)}, bf16[2,128,1024]{2,1,0:T(8,128)(2,1)}, u32[]{:S(2)}) copy-start(bf16[2,128,1024]{2,1,0:T(8,128)(2,1)} %param.5) | copy-start | bytes 1572868
  6.5 178.3 %copy-start.2 = (f32[1,2048]{1,0:T(1,128)S(1)}, f32[1,2048]{1,0:T(1,128)}, u32[]{:S(2)}) copy-start(f32[1,2048]{1,0:T(1,128)} %param.6) | copy-start | bytes 24580
  6.5 178.3 %all-gather.4.cloned.1.call-start = ((), (), s32[]{:S(2)}) async-start(), calls=%async_computation.3 | async-start | bytes 14155776 | tf_op jit(solution)/shard_map/all_gather | solution.py:61
  7.3 273.5 %all-gather.6.cloned.1.call-start = ((), (), s32[]{:S(2)}) async-start(), calls=%async_computation.4 | async-start | bytes 4718592 | tf_op jit(solution)/shard_map/all_gather | solution.py:62
  8.0 291.1 %reduce-scatter.4.cloned.1.call-start = ((), (), s32[]{:S(2)}) async-start(), calls=%async_computation.5 | async-start | bytes 786432 | tf_op jit(solution)/shard_map/reduce_scatter | solution.py:99
  187.7 31.0 %collective-permute-start.3 = (bf16[128,1024]{1,0:T(8,128)(2,1)S(1)}, bf16[128,1024]{1,0:T(8,128)(2,1)S(1)}, u32[]{:S(2)}, u32[]{:S(2)}) collective-permute-start(bf16[128,1024]{1,0:T(8,128)(2,1)S(1)} %fusion.36), channel_id=1, source_target_pairs={{0,8},{8,0},{2,10},{10,2},{4,12},{12,4},{6,14},{14,6},{1,9},{9,1},... | collective-permute-start | bytes 786440 | tf_op jit(solution)/shard_map/ppermute | solution.py:21
  190.8 40.7 %collective-permute-start = (bf16[128,1024]{1,0:T(8,128)(2,1)S(1)}, bf16[128,1024]{1,0:T(8,128)(2,1)S(1)}, u32[]{:S(2)}, u32[]{:S(2)}) collective-permute-start(bf16[128,1024]{1,0:T(8,128)(2,1)S(1)} %fusion.39), channel_id=1, source_target_pairs={{0,8},{8,0},{2,10},{10,2},{4,12},{12,4},{6,14},{14,6},{1,9},{9,1},... | collective-permute-start | bytes 786440 | tf_op jit(solution)/shard_map/ppermute | solution.py:21
  193.2 38.3 %collective-permute-start.1 = (bf16[128,1024]{1,0:T(8,128)(2,1)S(1)}, bf16[128,1024]{1,0:T(8,128)(2,1)}, u32[]{:S(2)}, u32[]{:S(2)}) collective-permute-start(bf16[128,1024]{1,0:T(8,128)(2,1)S(1)} %fusion.39), channel_id=1, source_target_pairs={{0,4},{4,0},{2,6},{6,2},{8,12},{12,8},{10,14},{14,10},{1,5},{5,1},... | collective-permute-start | bytes 786440 | tf_op jit(solution)/shard_map/ppermute | solution.py:21
  193.7 37.8 %collective-permute-start.2 = (bf16[128,1024]{1,0:T(8,128)(2,1)S(1)}, bf16[128,1024]{1,0:T(8,128)(2,1)}, u32[]{:S(2)}, u32[]{:S(2)}) collective-permute-start(bf16[128,1024]{1,0:T(8,128)(2,1)S(1)} %fusion.39), channel_id=1, source_target_pairs={{0,2},{2,0},{4,6},{6,4},{8,10},{10,8},{12,14},{14,12},{1,3},{3,1},... | collective-permute-start | bytes 786440 | tf_op jit(solution)/shard_map/ppermute | solution.py:21
  193.9 36.9 %collective-permute-start.4 = (bf16[128,1024]{1,0:T(8,128)(2,1)S(1)}, bf16[128,1024]{1,0:T(8,128)(2,1)S(1)}, u32[]{:S(2)}, u32[]{:S(2)}) collective-permute-start(bf16[128,1024]{1,0:T(8,128)(2,1)S(1)} %fusion.36), channel_id=1, source_target_pairs={{0,4},{4,0},{2,6},{6,2},{8,12},{12,8},{10,14},{14,10},{1,5},{5,1},... | collective-permute-start | bytes 786440 | tf_op jit(solution)/shard_map/ppermute | solution.py:21
  218.7 12.1 %collective-permute-start.5 = (bf16[128,1024]{1,0:T(8,128)(2,1)S(1)}, bf16[128,1024]{1,0:T(8,128)(2,1)S(1)}, u32[]{:S(2)}, u32[]{:S(2)}) collective-permute-start(bf16[128,1024]{1,0:T(8,128)(2,1)S(1)} %fusion.36), channel_id=1, source_target_pairs={{0,2},{2,0},{4,6},{6,4},{8,10},{10,8},{12,14},{14,12},{1,3},{3,1},... | collective-permute-start | bytes 786440 | tf_op jit(solution)/shard_map/ppermute | solution.py:21
  230.9 1.0 copy-start.4
  284.5 89.1 %reduce-scatter.6.cloned.1.call-start = ((), (), s32[]{:S(2)}) async-start(), calls=%async_computation.6 | async-start | bytes 786432 | tf_op jit(solution)/shard_map/reduce_scatter | solution.py:99
  300.1 3.4 collective-permute-start.6
  315.3 20.5 %collective-permute-start.10 = (bf16[128,1024]{1,0:T(8,128)(2,1)S(1)}, bf16[128,1024]{1,0:T(8,128)(2,1)S(1)}, u32[]{:S(2)}, u32[]{:S(2)}) collective-permute-start(bf16[128,1024]{1,0:T(8,128)(2,1)S(1)} %fusion.37), channel_id=1, source_target_pairs={{0,8},{8,0},{2,10},{10,2},{4,12},{12,4},{6,14},{14,6},{1,9},{9,1},... | collective-permute-start | bytes 786440 | tf_op jit(solution)/shard_map/ppermute | solution.py:21
  318.6 25.9 %collective-permute-start.7 = (bf16[128,1024]{1,0:T(8,128)(2,1)S(1)}, bf16[128,1024]{1,0:T(8,128)(2,1)}, u32[]{:S(2)}, u32[]{:S(2)}) collective-permute-start(bf16[128,1024]{1,0:T(8,128)(2,1)S(1)} %fusion.40), channel_id=1, source_target_pairs={{0,8},{8,0},{2,10},{10,2},{4,12},{12,4},{6,14},{14,6},{1,9},{9,1},... | collective-permute-start | bytes 786440 | tf_op jit(solution)/shard_map/ppermute | solution.py:21
  320.8 23.7 %collective-permute-start.8 = (bf16[128,1024]{1,0:T(8,128)(2,1)S(1)}, bf16[128,1024]{1,0:T(8,128)(2,1)}, u32[]{:S(2)}, u32[]{:S(2)}) collective-permute-start(bf16[128,1024]{1,0:T(8,128)(2,1)S(1)} %fusion.40), channel_id=1, source_target_pairs={{0,4},{4,0},{2,6},{6,2},{8,12},{12,8},{10,14},{14,10},{1,5},{5,1},... | collective-permute-start | bytes 786440 | tf_op jit(solution)/shard_map/ppermute | solution.py:21
  321.1 23.5 %collective-permute-start.9 = (bf16[128,1024]{1,0:T(8,128)(2,1)S(1)}, bf16[128,1024]{1,0:T(8,128)(2,1)}, u32[]{:S(2)}, u32[]{:S(2)}) collective-permute-start(bf16[128,1024]{1,0:T(8,128)(2,1)S(1)} %fusion.40), channel_id=1, source_target_pairs={{0,2},{2,0},{4,6},{6,4},{8,10},{10,8},{12,14},{14,12},{1,3},{3,1},... | collective-permute-start | bytes 786440 | tf_op jit(solution)/shard_map/ppermute | solution.py:21
  322.2 21.6 %collective-permute-start.11 = (bf16[128,1024]{1,0:T(8,128)(2,1)S(1)}, bf16[128,1024]{1,0:T(8,128)(2,1)S(1)}, u32[]{:S(2)}, u32[]{:S(2)}) collective-permute-start(bf16[128,1024]{1,0:T(8,128)(2,1)S(1)} %fusion.37), channel_id=1, source_target_pairs={{0,4},{4,0},{2,6},{6,2},{8,12},{12,8},{10,14},{14,10},{1,5},{5,1},... | collective-permute-start | bytes 786440 | tf_op jit(solution)/shard_map/ppermute | solution.py:21
  335.8 8.1 %collective-permute-start.12 = (bf16[128,1024]{1,0:T(8,128)(2,1)S(1)}, bf16[128,1024]{1,0:T(8,128)(2,1)S(1)}, u32[]{:S(2)}, u32[]{:S(2)}) collective-permute-start(bf16[128,1024]{1,0:T(8,128)(2,1)S(1)} %fusion.37), channel_id=1, source_target_pairs={{0,2},{2,0},{4,6},{6,4},{8,10},{10,8},{12,14},{14,12},{1,3},{3,1},... | collective-permute-start | bytes 786440 | tf_op jit(solution)/shard_map/ppermute | solution.py:21
  344.5 3.1 copy-start.5
  357.2 90.4 %reduce-scatter.8.cloned.1.call-start = ((), (), s32[]{:S(2)}) async-start(), calls=%async_computation.7 | async-start | bytes 786432 | tf_op jit(solution)/shard_map/reduce_scatter | solution.py:99
  374.7 3.4 collective-permute-start.13
  389.7 20.4 %collective-permute-start.17 = (bf16[128,1024]{1,0:T(8,128)(2,1)S(1)}, bf16[128,1024]{1,0:T(8,128)(2,1)S(1)}, u32[]{:S(2)}, u32[]{:S(2)}) collective-permute-start(bf16[128,1024]{1,0:T(8,128)(2,1)S(1)} %fusion.38), channel_id=1, source_target_pairs={{0,8},{8,0},{2,10},{10,2},{4,12},{12,4},{6,14},{14,6},{1,9},{9,1},... | collective-permute-start | bytes 786440 | tf_op jit(solution)/shard_map/ppermute | solution.py:21
  393.0 25.9 %collective-permute-start.14 = (bf16[128,1024]{1,0:T(8,128)(2,1)S(1)}, bf16[128,1024]{1,0:T(8,128)(2,1)S(1)}, u32[]{:S(2)}, u32[]{:S(2)}) collective-permute-start(bf16[128,1024]{1,0:T(8,128)(2,1)S(1)} %fusion.41), channel_id=1, source_target_pairs={{0,8},{8,0},{2,10},{10,2},{4,12},{12,4},{6,14},{14,6},{1,9},{9,1},... | collective-permute-start | bytes 786440 | tf_op jit(solution)/shard_map/ppermute | solution.py:21
  395.2 23.7 %collective-permute-start.15 = (bf16[128,1024]{1,0:T(8,128)(2,1)S(1)}, bf16[128,1024]{1,0:T(8,128)(2,1)}, u32[]{:S(2)}, u32[]{:S(2)}) collective-permute-start(bf16[128,1024]{1,0:T(8,128)(2,1)S(1)} %fusion.41), channel_id=1, source_target_pairs={{0,4},{4,0},{2,6},{6,2},{8,12},{12,8},{10,14},{14,10},{1,5},{5,1},... | collective-permute-start | bytes 786440 | tf_op jit(solution)/shard_map/ppermute | solution.py:21
  395.4 23.5 %collective-permute-start.16 = (bf16[128,1024]{1,0:T(8,128)(2,1)S(1)}, bf16[128,1024]{1,0:T(8,128)(2,1)}, u32[]{:S(2)}, u32[]{:S(2)}) collective-permute-start(bf16[128,1024]{1,0:T(8,128)(2,1)S(1)} %fusion.41), channel_id=1, source_target_pairs={{0,2},{2,0},{4,6},{6,4},{8,10},{10,8},{12,14},{14,12},{1,3},{3,1},... | collective-permute-start | bytes 786440 | tf_op jit(solution)/shard_map/ppermute | solution.py:21
  396.6 21.6 %collective-permute-start.18 = (bf16[128,1024]{1,0:T(8,128)(2,1)S(1)}, bf16[128,1024]{1,0:T(8,128)(2,1)S(1)}, u32[]{:S(2)}, u32[]{:S(2)}) collective-permute-start(bf16[128,1024]{1,0:T(8,128)(2,1)S(1)} %fusion.38), channel_id=1, source_target_pairs={{0,4},{4,0},{2,6},{6,2},{8,12},{12,8},{10,14},{14,10},{1,5},{5,1},... | collective-permute-start | bytes 786440 | tf_op jit(solution)/shard_map/ppermute | solution.py:21
  410.1 8.1 %collective-permute-start.19 = (bf16[128,1024]{1,0:T(8,128)(2,1)S(1)}, bf16[128,1024]{1,0:T(8,128)(2,1)S(1)}, u32[]{:S(2)}, u32[]{:S(2)}) collective-permute-start(bf16[128,1024]{1,0:T(8,128)(2,1)S(1)} %fusion.38), channel_id=1, source_target_pairs={{0,2},{2,0},{4,6},{6,4},{8,10},{10,8},{12,14},{14,12},{1,3},{3,1},... | collective-permute-start | bytes 786440 | tf_op jit(solution)/shard_map/ppermute | solution.py:21
  418.8 3.0 copy-start.3
Sparse Core Ops, SparseCore 0:
  9.5 175.2 all-gather.3
  186.8 93.8 all-gather.5
  284.6 14.4 reduce-scatter.3
  357.3 16.1 reduce-scatter.5
  431.4 16.1 reduce-scatter.7
where the time goes:
time: 459 us; the launch traced here: 456 us
  waiting for transfers between devices  316 us (69%)
  matrix products  66 us (14%)
  blocking collectives  24.8 us (5%)
  between operations  21.2 us (5%)
  starting transfers between devices  19.9 us (4%)
  other arithmetic  5.15 us (1%)
    all_gather x1, waiting for transfers between devices, local(): lax.all_gather(w_qkv, 'node', axis=2, tiled=True)  165 us
    ppermute x18, waiting for transfers between devices, from_partner(): return lax.ppermute(block, axis, route)  63.1 us
    reduce_scatter x3, waiting for transfers between devices, local(): lax.psum_scatter(terms.astype(jnp.bfloat16), 'head', scatter_dimension=1,...  42.3 us
    all_gather x1, waiting for transfers between devices, local(): lax.all_gather(w_out, 'node', axis=2, tiled=True)  40.2 us
    all_gather x3, blocking collectives, local(): whole = lax.all_gather(inputs, 'head', axis=1, tiled=True)  24.8 us
    ppermute x18, starting transfers between devices, from_partner(): return lax.ppermute(block, axis, route)  17.1 us
    dot_general x3, matrix products, partial_attend(): jnp.einsum('hqk,khd->hqd', expo.astype(jnp.bfloat16), v_heads, preferred_...  11.3 us
    dot_general x3, matrix products, local(): terms = jnp.dot(attended, w_proj, preferred_element_type=jnp.float32)  11.2 us
  transfers between devices with their start and end apart: 25, of which 13 were waited for; matrix products, arithmetic and copies ran while one was open for 8% of the time, Pallas kernels for 0%

commit v1 on v0

--- a/solution.py
+++ b/solution.py
@@ -1,6 +1,9 @@
+import functools
 import jax
 import jax.numpy as jnp
 from jax import lax
+from jax.experimental import pallas as pl
+from jax.experimental.pallas import tpu as pltpu
 from jax.sharding import PartitionSpec as P
 
 HD = 128
@@ -52,7 +55,7 @@
     return jnp.transpose(out, (1, 0, 2)).reshape(rows, -1).astype(jnp.bfloat16)
 
 
-def local(feats, gain, w_qkv, w_out, block_mask):
+def local_any(feats, gain, w_qkv, w_out, block_mask):
     segment = lax.axis_index("pipe")
     me = lax.axis_index("node")
     width = lax.axis_size("node").bit_length() - 1
@@ -108,9 +111,419 @@
     return jnp.stack([first, second])[None]
 
 
+MESH_ID = pl.DeviceIdType.MESH
+ANY = pl.BlockSpec(memory_space=pl.ANY)
+
+
+def place():
+    core, node, y = lax.axis_index("pipe"), lax.axis_index("node"), lax.axis_index("head")
+    return core, lax.rem(node, 2), y, lax.div(node, 2)
+
+
+def dev(core, x, y, z):
+    return (core, z * 2 + x, y)
+
+
+def z_apart(z, d):
+    if d == 0:
+        return z
+    if d == 1:
+        return z + 1 - 2 * lax.rem(z, 2)
+    if d == 2:
+        return z + 2 - 4 * lax.div(z, 2)
+    return 3 - z
+
+
+def remote(src, dst, send, recv, target):
+    return pltpu.make_async_remote_copy(
+        src_ref=src, dst_ref=dst, send_sem=send, recv_sem=recv, device_id=target, device_id_type=MESH_ID
+    )
+
+
+def greet(peers):
+    barrier = pltpu.get_barrier_semaphore()
+    for peer in peers:
+        pl.semaphore_signal(barrier, inc=1, device_id=peer, device_id_type=MESH_ID)
+    pl.semaphore_wait(barrier, len(peers))
+
+
+def head_slot(core, y, z):
+    return 8 * y + 2 * z + core
+
+
+def column_slot(core, y, z):
+    return 4 * z + 2 * y + core
+
+
+def columns_kernel(slot, own, out, local_sem, z_send, z_recv, y_send, y_recv, b_send, b_recv):
+    core, x, y, z = place()
+    wide = own.shape[1]
+
+    def region(c, yy, zz):
+        return out.at[:, pl.ds(pl.multiple_of(slot(c, yy, zz) * wide, wide), wide)]
+
+    far = [dev(core, x, y, z_apart(z, d)) for d in (1, 2, 3)]
+    beside, sibling = dev(core, x, 1 - y, z), dev(1 - core, x, y, z)
+    greet(far + [beside, sibling])
+    sent = []
+
+    def send(src, dst, ssem, rsem, target):
+        copy = remote(src, dst, ssem, rsem, target)
+        copy.start()
+        sent.append(copy)
+
+    mine = region(core, y, z)
+    send(own, mine, y_send.at[0], y_recv.at[0], beside)
+    for d in (3, 2, 1):
+        send(own, mine, z_send.at[d - 1], z_recv.at[d - 1], far[d - 1])
+    send(own, mine, b_send.at[0], b_recv.at[0], sibling)
+    keep = pltpu.make_async_copy(own, mine, local_sem)
+    keep.start()
+    for d in (1, 2, 3):
+        got = region(core, y, z_apart(z, d))
+        remote(own, got, z_send.at[d - 1], z_recv.at[d - 1], sibling).wait_recv()
+        send(got, got, y_send.at[d], y_recv.at[d], beside)
+        send(got, got, b_send.at[d], b_recv.at[d], sibling)
+    for d in range(4):
+        got = region(core, 1 - y, z_apart(z, d))
+        remote(own, got, y_send.at[d], y_recv.at[d], sibling).wait_recv()
+        send(got, got, b_send.at[4 + d], b_recv.at[4 + d], sibling)
+    for d in range(8):
+        got = region(1 - core, y if d < 4 else 1 - y, z_apart(z, d % 4))
+        remote(own, got, b_send.at[d], b_recv.at[d], sibling).wait_recv()
+    for copy in sent:
+        copy.wait_send()
+    keep.wait()
+
+
+def all_columns(own, slot, ident):
+    dma = pltpu.SemaphoreType.DMA
+    return pl.pallas_call(
+        functools.partial(columns_kernel, slot),
+        out_shape=jax.ShapeDtypeStruct((own.shape[0], own.shape[1] * 16), own.dtype),
+        in_specs=[ANY],
+        out_specs=ANY,
+        scratch_shapes=[dma(()), dma((3,)), dma((3,)), dma((4,)), dma((4,)), dma((8,)), dma((8,))],
+        compiler_params=pltpu.CompilerParams(collective_id=ident, has_side_effects=True),
+        name="all_columns_%d" % ident,
+    )(own)
+
+
+def spread_kernel(
+    feats, gain, w_qkv, w_out, xg, gains, wq, wo,
+    l_sem, x_send, x_recv, z_send, z_recv, y_send, y_recv, b_send, b_recv,
+    g_send, g_recv, q_send, q_recv, qx_send, qx_recv, o_send, o_recv,
+):
+    core, x, y, z = place()
+    node = z * 2 + x
+    half, wide = feats.shape[1] // 2, feats.shape[2]
+    depth = w_qkv.shape[2]
+    far = [z_apart(z, d) for d in (1, 2, 3)]
+    beside, sibling, across = dev(core, x, 1 - y, z), dev(1 - core, x, y, z), dev(core, 1 - x, y, z)
+    plane = [
+        dev(cc, xx, yy, z)
+        for cc in (core, 1 - core)
+        for xx in (x, 1 - x)
+        for yy in (y, 1 - y)
+    ][1:]
+    greet(plane + [dev(cc, x, y, zz) for zz in far for cc in (core, 1 - core)])
+    sent = []
+    local = []
+
+    def send(src, dst, ssem, rsem, target):
+        copy = remote(src, dst, ssem, rsem, target)
+        copy.start()
+        sent.append(copy)
+
+    def keep(src, dst, sem):
+        copy = pltpu.make_async_copy(src, dst, sem)
+        copy.start()
+        local.append(copy)
+
+    def region(c, xx, yy, zz):
+        return xg.at[
+            pl.ds(pl.multiple_of((zz * 2 + xx) * 2 * half + c * half, half), half),
+            pl.ds(pl.multiple_of(yy * wide, wide), wide),
+        ]
+
+    rows = pl.ds(pl.multiple_of(core * half, half), half)
+    mine, other = feats.at[x, rows, :], feats.at[1 - x, rows, :]
+    spot = region(core, x, y, z)
+    send(other, spot, x_send, x_recv, across)
+    send(mine, spot, y_send.at[0], y_recv.at[0], beside)
+    for d in (3, 2, 1):
+        send(mine, spot, z_send.at[d - 1], z_recv.at[d - 1], dev(core, x, y, far[d - 1]))
+    send(mine, spot, b_send.at[0], b_recv.at[0], sibling)
+    keep(mine, spot, l_sem.at[0])
+    send(gain, gains.at[core], g_send, g_recv, sibling)
+    keep(gain, gains.at[core], l_sem.at[1])
+
+    def head_columns(zz, c):
+        return w_qkv.at[0, :, :, pl.ds(pl.multiple_of((zz * 2 + c) * HD, HD), HD)]
+
+    def depth_rows(c, xx, zz):
+        return wq.at[c, :, pl.ds(pl.multiple_of((zz * 2 + xx) * depth, depth), depth), :]
+
+    own_rows = depth_rows(core, x, z)
+    for d in (0, 3, 2, 1):
+        zz = z_apart(z, d)
+        for other_core in range(2):
+            target = 1 - core if other_core else core
+            if d == 0 and not other_core:
+                keep(head_columns(z, core), own_rows, l_sem.at[2])
+                send(head_columns(z, core), own_rows, qx_send.at[0], qx_recv.at[0], across)
+            else:
+                at = 2 * d + other_core
+                send(head_columns(zz, target), own_rows, q_send.at[at], q_recv.at[at], dev(target, x, y, zz))
+
+    half_rows = w_out.shape[1]
+    to = wo.at[core, pl.ds(pl.multiple_of(y * half_rows, half_rows), half_rows), :]
+    projections = []
+    for a in range(2):
+        for b in range(2):
+            xx = 1 - x if a else x
+            cc = 1 - core if b else core
+            src = w_out.at[0, :, pl.ds(pl.multiple_of(cc * HD, HD), HD)]
+            rsem = o_recv.at[2 * y + core]
+            copy = remote(src, to, o_send.at[2 * a + b], rsem, dev(cc, xx, x, z))
+            if a == 0 and b == 0:
+                pl.when(x != y)(copy.start)
+                pl.when(x == y)(pltpu.make_async_copy(src, to, rsem).start)
+            else:
+                copy.start()
+            projections.append(copy)
+
+    far_x = region(core, 1 - x, y, z)
+    remote(mine, far_x, x_send, x_recv, sibling).wait_recv()
+    send(far_x, far_x, y_send.at[4], y_recv.at[4], beside)
+    for d in (3, 2, 1):
+        send(far_x, far_x, z_send.at[2 + d], z_recv.at[2 + d], dev(core, x, y, far[d - 1]))
+    send(far_x, far_x, b_send.at[8], b_recv.at[8], sibling)
+    for k in range(2):
+        xx = 1 - x if k else x
+        for d in (1, 2, 3):
+            got = region(core, xx, y, far[d - 1])
+            remote(mine, got, x_send, z_recv.at[3 * k + d - 1], sibling).wait_recv()
+            send(got, got, y_send.at[4 * k + d], y_recv.at[4 * k + d], beside)
+            send(got, got, b_send.at[8 * k + d], b_recv.at[8 * k + d], sibling)
+    for d in range(4):
+        for other_core in range(2):
+            at = 2 * d + other_core
+            if at == 0:
+                continue
+            got = depth_rows(1 - core if other_core else core, x, z_apart(z, d))
+            remote(head_columns(z, core), got, x_send, q_recv.at[at], sibling).wait_recv()
+            send(got, got, qx_send.at[at], qx_recv.at[at], across)
+    for k in range(2):
+        xx = 1 - x if k else x
+        for d in range(4):
+            got = region(core, xx, 1 - y, z_apart(z, d))
+            remote(mine, got, x_send, y_recv.at[4 * k + d], sibling).wait_recv()
+            send(got, got, b_send.at[8 * k + 4 + d], b_recv.at[8 * k + 4 + d], sibling)
+    for k in range(2):
+        xx = 1 - x if k else x
+        for d in range(8):
+            got = region(1 - core, xx, y if d < 4 else 1 - y, z_apart(z, d % 4))
+            remote(mine, got, x_send, b_recv.at[8 * k + d], sibling).wait_recv()
+    for d in range(4):
+        for other_core in range(2):
+            at = 2 * d + other_core
+            got = depth_rows(1 - core if other_core else core, 1 - x, z_apart(z, d))
+            remote(head_columns(z, core), got, x_send, qx_recv.at[at], sibling).wait_recv()
+    remote(gain, gains.at[1 - core], g_send, g_recv, sibling).wait_recv()
+    for yy in range(2):
+        for cc in range(2):
+            got = wo.at[cc, pl.ds(yy * half_rows, half_rows), :]
+            remote(w_out.at[0, :, pl.ds(0, HD)], got, x_send, o_recv.at[2 * yy + cc], sibling).wait_recv()
+    for copy in sent:
+        copy.wait_send()
+    for copy in local:
+        copy.wait()
+    pl.when(x != y)(projections[0].wait_send)
+    for copy in projections[1:]:
+        copy.wait_send()
+
+
+def spread(feats, gain, w_qkv, w_out):
+    dma = pltpu.SemaphoreType.DMA
+    bf = jnp.bfloat16
+    rows, wide = feats.shape[1] * 8, feats.shape[2] * 2
+    return pl.pallas_call(
+        spread_kernel,
+        out_shape=(
+            jax.ShapeDtypeStruct((rows, wide), bf),
+            jax.ShapeDtypeStruct((2, 1, wide), jnp.float32),
+            jax.ShapeDtypeStruct((2, 3, wide, HD), bf),
+            jax.ShapeDtypeStruct((2, wide, HD), bf),
+        ),
+        in_specs=[ANY] * 4,
+        out_specs=(ANY,) * 4,
+        scratch_shapes=[dma((3,)), dma(()), dma(()), dma((6,)), dma((6,)), dma((8,)), dma((8,)), dma((16,)), dma((16,)),
+                        dma(()), dma(()), dma((8,)), dma((8,)), dma((8,)), dma((8,)), dma((4,)), dma((4,))],
+        compiler_params=pltpu.CompilerParams(collective_id=0, has_side_effects=True),
+        name="spread",
+    )(feats, gain, w_qkv, w_out)
+
+
+def deliver_kernel(mid, last, out, l_sem, m_send, m_recv, a_send, a_recv):
+    core, x, y, z = place()
+    node = z * 2 + x
+    rows, wide = out.shape[1], out.shape[2]
+    piece = last.shape[1]
+    to_y = lax.div(z, 2)
+    z_low = lax.rem(z, 2)
+    first = core == 0
+    to_self = (core == 1) & (y == to_y)
+    barrier = pltpu.get_barrier_semaphore()
+
+    def signal(peer):
+        pl.semaphore_signal(barrier, inc=1, device_id=peer, device_id_type=MESH_ID)
+
+    @pl.when(first)
+    def _():
+        signal(dev(0, 1 - x, y, z))
+
+    sources = [(zl, xx, yy, cc) for zl in range(2) for xx in range(2) for yy in range(2) for cc in range(2)]
+    for zl, xx, yy, cc in sources:
+        own = (cc == core) & (xx == x) & (yy == y) & (2 * y + zl == z)
+
+        @pl.when((core == 1) & jnp.logical_not(own))
+        def _():
+            signal(dev(cc, xx, yy, 2 * y + zl))
+
+    pl.semaphore_wait(barrier, 8 - to_self.astype(jnp.int32) + first.astype(jnp.int32))
+
+    def mid_rows(n):
+        return mid.at[
+            pl.ds(pl.multiple_of(n * rows, rows), rows), pl.ds(pl.multiple_of(y * wide, wide), wide)
+        ]
+
+    cross = remote(mid_rows(z * 2 + 1 - x), out.at[x], m_send, m_recv, dev(0, 1 - x, y, z))
+    keep = pltpu.make_async_copy(mid_rows(node), out.at[x], l_sem)
+
+    @pl.when(first)
+    def _():
+        cross.start()
+        keep.start()
+
+    slot = 4 * z_low + 2 * y + core
+    spot = out.at[x, :, pl.ds(pl.multiple_of(slot * piece, piece), piece)]
+    index = 8 * z_low + 4 * x + 2 * y + core
+    copies = []
+    for n in range(8):
+        src = last.at[pl.ds(n * rows, rows), :]
+        copy = remote(src, spot, a_send.at[n], a_recv.at[index], dev(1, n % 2, to_y, n // 2))
+        own = to_self & (node == n)
+        pl.when(jnp.logical_not(own))(copy.start)
+        pl.when(own)(pltpu.make_async_copy(src, spot, a_recv.at[index]).start)
+        copies.append((copy, own))
+
+    @pl.when(first)
+    def _():
+        remote(mid_rows(node), out.at[1 - x], m_send, m_recv, dev(0, 1 - x, y, z)).wait_recv()
+        cross.wait_send()
+        keep.wait()
+
+    @pl.when(core == 1)
+    def _():
+        for zl, xx, yy, cc in sources:
+            at = 4 * zl + 2 * yy + cc
+            got = out.at[xx, :, pl.ds(at * piece, piece)]
+            remote(
+                last.at[pl.ds(0, rows), :], got, a_send.at[0], a_recv.at[8 * zl + 4 * xx + 2 * yy + cc],
+                dev(0, x, y, z),
+            ).wait_recv()
+
+    for copy, own in copies:
+        pl.when(jnp.logical_not(own))(copy.wait_send)
+
+
+def deliver(mid, last):
+    dma = pltpu.SemaphoreType.DMA
+    return pl.pallas_call(
+        deliver_kernel,
+        out_shape=jax.ShapeDtypeStruct((2, mid.shape[0] // 8, mid.shape[1] // 2), mid.dtype),
+        in_specs=[ANY] * 2,
+        out_specs=ANY,
+        scratch_shapes=[dma(()), dma(()), dma(()), dma((8,)), dma((16,))],
+        compiler_params=pltpu.CompilerParams(collective_id=3, has_side_effects=True),
+        name="deliver",
+    )(mid, last)
+
+
+def attend_kernel(x_ref, gain_ref, w_ref, flags, out_ref, q_ref, k_ref, v_ref):
+    count = flags.shape[0]
+    rows = x_ref.shape[0] // count
+    step = 2 * rows
+    width = count.bit_length() - 1
+    bits = [width - 1, width // 2, 0]
+
+    def project(at, _):
+        span = pl.ds(pl.multiple_of(at * step, step), step)
+        xf = x_ref[span, :].astype(jnp.float32)
+        inv = lax.rsqrt(jnp.mean(xf * xf, axis=-1, keepdims=True) + EPS)
+        normed = (xf * inv * gain_ref[...]).astype(jnp.bfloat16)
+        for part, ref in enumerate((q_ref, k_ref, v_ref)):
+            ref[span, :] = jnp.dot(normed, w_ref[part], preferred_element_type=jnp.float32).astype(jnp.bfloat16)
+        return 0
+
+    lax.fori_loop(0, x_ref.shape[0] // step, project, 0)
+    for block in range(count):
+        seen = [block] + [block ^ (1 << bit) for bit in bits]
+        span = slice(block * rows, (block + 1) * rows)
+        query = q_ref[span, :]
+        scores = []
+        for other in seen:
+            key = k_ref[other * rows : (other + 1) * rows, :]
+            dots = lax.dot_general(query, key, (((1,), (1,)), ((), ())), preferred_element_type=jnp.float32)
+            scores.append(jnp.where(flags[block, other] > 0, dots * (1.0 / HD**0.5), NEG))
+        top = functools.reduce(jnp.maximum, [jnp.max(s, axis=-1, keepdims=True) for s in scores])
+        total = jnp.zeros_like(top)
+        summed = jnp.zeros((rows, HD), jnp.float32)
+        for other, s in zip(seen, scores):
+            expo = jnp.where(flags[block, other] > 0, jnp.exp(s - top), 0.0)
+            total = total + jnp.sum(expo, axis=-1, keepdims=True)
+            summed = summed + jnp.dot(
+                expo.astype(jnp.bfloat16), v_ref[other * rows : (other + 1) * rows, :],
+                preferred_element_type=jnp.float32,
+            )
+        out_ref[span, :] = (summed / total).astype(jnp.bfloat16)
+
+
+def attend(x, gain_row, w, flags):
+    vmem = pl.BlockSpec(memory_space=pltpu.VMEM)
+    rows = x.shape[0]
+    return pl.pallas_call(
+        attend_kernel,
+        out_shape=jax.ShapeDtypeStruct((rows, HD), jnp.bfloat16),
+        in_specs=[vmem, vmem, vmem, pl.BlockSpec(memory_space=pltpu.SMEM)],
+        out_specs=vmem,
+        scratch_shapes=[pltpu.VMEM((rows, HD), jnp.bfloat16)] * 3,
+        compiler_params=pltpu.CompilerParams(vmem_limit_bytes=40 * 2**20),
+        name="attend",
+    )(x, gain_row, w, flags)
+
+
+def local_planes(feats, gain, w_qkv, w_out, block_mask):
+    core, micro, y, z = place()
+    flags = lax.dynamic_index_in_dim(block_mask, micro, 0, keepdims=False)
+    whole, gains, wq, wo = spread(feats, gain, w_qkv, w_out)
+    column = column_slot(core, y, z) * HD
+
+    def layer(x, s):
+        attended = all_columns(attend(x, gains[s], wq[s], flags), head_slot, 1)
+        projected = jnp.dot(attended, wo[s], preferred_element_type=jnp.float32)
+        residual = lax.dynamic_slice_in_dim(x, column, HD, axis=1)
+        return (residual.astype(jnp.float32) + projected).astype(jnp.bfloat16)
+
+    mid = all_columns(layer(whole, 0), column_slot, 2)
+    return deliver(mid, layer(mid, 1))[None]
+
+
 def solution(mesh):
+    planes = (mesh.shape["pipe"], mesh.shape["node"], mesh.shape["head"]) == (2, 8, 2)
     return jax.shard_map(
-        local,
+        local_planes if planes else local_any,
         mesh=mesh,
         in_specs=(
             P(None, "node", "head"),

time: 459 us -> 267 us (0.58)
  waiting for transfers between devices: 316 us -> 0 us
  Pallas kernels: 0 us -> 245 us
  matrix products: 66 us -> 8.38 us
  blocking collectives: 24.8 us -> 0 us
  between operations: 21.2 us -> 0.15 us
  starting transfers between devices: 19.9 us -> 0 us
  local copies, waits for them, and re-layouts: 2.96 us -> 10.4 us
  other arithmetic: 5.15 us -> 0 us
    pallas_call x0 -> x7, Pallas kernels: none -> 245 us  [the longest x3 125 us: all_columns(): pl.pallas_call(functools.partial(columns_kernel, slot), out_shape=jax.Sha...]
    all_gather x2 -> x0, waiting for transfers between devices: 205 us -> none  [the longest x1 165 us: local(): lax.all_gather(w_qkv, 'node', axis=2, tiled=True)]
    ppermute x20 -> x0, waiting for transfers between devices: 67.1 us -> none  [the longest x18 63.1 us: from_partner(): return lax.ppermute(block, axis, route)]
    dot_general x18 -> x2, matrix products: 60 us -> 8.38 us  [layer(): projected = jnp.dot(attended, wo[s], preferred_element_type=jnp.float32)]
    reduce_scatter x3 -> x0, waiting for transfers between devices: 42.3 us -> none  [local(): lax.psum_scatter(terms.astype(jnp.bfloat16), 'head', scatter_dimension=1,...]
    all_gather x3 -> x0, blocking collectives: 24.8 us -> none  [local(): whole = lax.all_gather(inputs, 'head', axis=1, tiled=True)]
    ppermute x20 -> x0, starting transfers between devices: 19.7 us -> none  [the longest x18 17.1 us: from_partner(): return lax.ppermute(block, axis, route)]
    unnamed x12 -> x13, local copies, waits for them, and re-layouts: 0.39 us -> 7.63 us
  transfers between devices with their start and end apart: 25 -> 0, of which waited for: 13 -> 0; matrix products, arithmetic and copies ran while one was open for 8% -> 0% of each run, Pallas kernels for 0% -> 0%
where the time goes in v1:
time: 267 us; the launch traced here: 264 us
  Pallas kernels  245 us (92%)
  local copies, waits for them, and re-layouts  10.4 us (4%)
  matrix products  8.38 us (3%)
    pallas_call x3, Pallas kernels, all_columns(): pl.pallas_call(functools.partial(columns_kernel, slot), out_shape=jax.Sha...  125 us
    pallas_call x1, Pallas kernels, spread(): pl.pallas_call(spread_kernel, out_shape=(jax.ShapeDtypeStruct((rows, wide...  92.3 us
    pallas_call x2, Pallas kernels, attend(): pl.pallas_call(attend_kernel, out_shape=jax.ShapeDtypeStruct((rows, HD),...  16.7 us
    pallas_call x1, Pallas kernels, deliver(): pl.pallas_call(deliver_kernel, out_shape=jax.ShapeDtypeStruct((2, mid.sha...  11 us
    dot_general x2, matrix products, layer(): projected = jnp.dot(attended, wo[s], preferred_element_type=jnp.float32)  8.38 us
    unnamed x13, local copies, waits for them, and re-layouts  7.63 us

profile of v1, /device:TPU:25, one launch (start us, length us, event | category | flops | bytes accessed | tf_op | source)
XLA Modules:
  0.0 263.5 jit_solution(17392515296402459431)
XLA Ops:
  0.0 0.0 copy-start
  0.0 92.3 %spread.1 = (bf16[1024,2048]{1,0:T(8,128)(2,1)}, f32[2,1,2048]{2,1,0:T(1,128)}, bf16[2,3,2048,128]{3,2,1,0:T(8,128)(2,1)}, bf16[2,2048,128]{2,1,0:T(8,128)(2,1)}) custom-call(bf16[2,128,1024]{2,1,0:T(8,128)(2,1)} %feats.1, f32[1,2048]{1,0:T(1,128)} %gain.1, bf16[1,3,256,1024]{3,2,1,0:T(8,128)(2,1)} %w_qkv.1, bf16[1,1024,256]{2,1,0:T(8,128)(2,1)} %w_out.1), custom_call_target="tpu_custom_call" | custom-call | tf_op jit(solution)/shard_map/spread/pallas_call | solution.py:351
  92.3 0.7 slice_bitcast_fusion.2
  93.1 2.1 slice_bitcast_fusion
  95.2 0.0 copy-done
  95.2 0.0 copy-start.2
  95.2 2.2 copy-done.2
  97.4 8.5 %attend.2.own = bf16[1024,128]{1,0:T(8,128)(2,1)S(1)} custom-call(bf16[1024,2048]{1,0:T(8,128)(2,1)S(1)} %copy-done.2, f32[1,2048]{1,0:T(1,128)S(1)} %get-tuple-element.16.gain_ref, bf16[3,2048,128]{2,1,0:T(8,128)(2,1)S(1)} %get-tuple-element.14.w_ref, s32[8,8]{1,0:T(8,128)S(1)} %dynamic-slice_bitcast_fusion.flags), custom_call_target="tpu_custom_call" | custom-call | tf_op jit(solution)/shard_map/attend/pallas_call | solution.py:496
  105.9 0.0 copy-start.4
  105.9 0.7 copy-done.4
  106.6 0.0 copy-start.5
  106.6 41.7 %all_columns_1.2 = bf16[1024,2048]{1,0:T(8,128)(2,1)} custom-call(bf16[1024,128]{1,0:T(8,128)(2,1)} %copy-done.4), custom_call_target="tpu_custom_call" | custom-call | tf_op jit(solution)/shard_map/all_columns_1/pallas_call | solution.py:201
  148.3 0.0 copy-done.5
  148.3 4.2 %fusion.own = bf16[1024,128]{1,0:T(8,128)(2,1)} fusion(bf16[1024,2048]{1,0:T(8,128)(2,1)} %all_columns_1.2, bf16[2,2048,128]{2,1,0:T(8,128)(2,1)S(1)} %copy-done.5, bf16[1024,2048]{1,0:T(8,128)(2,1)} %get-tuple-element.9.x_ref, s32[]{:T(128)S(6)} %select_n.8), kind=kOutput, calls=%fused_computation.4 | convolution fusion | flops 537264128 | bytes 5242884 | tf_op jit(solution)/shard_map/dot_general | solution.py:515
  152.5 40.7 %all_columns_2.1.x_ref.mid = bf16[1024,2048]{1,0:T(8,128)(2,1)} custom-call(bf16[1024,128]{1,0:T(8,128)(2,1)} %fusion.own), custom_call_target="tpu_custom_call" | custom-call | tf_op jit(solution)/shard_map/all_columns_2/pallas_call | solution.py:201
  193.2 0.0 copy-start.1
  193.2 2.2 copy-done.1
  195.4 8.2 %attend.3.own = bf16[1024,128]{1,0:T(8,128)(2,1)S(1)} custom-call(bf16[1024,2048]{1,0:T(8,128)(2,1)S(1)} %copy-done.1, f32[1,2048]{1,0:T(1,128)S(1)} %get-tuple-element.15.gain_ref, bf16[3,2048,128]{2,1,0:T(8,128)(2,1)S(1)} %get-tuple-element.13.w_ref, s32[8,8]{1,0:T(8,128)S(1)} %dynamic-slice_bitcast_fusion.flags), custom_call_target="tpu_custom_call" | custom-call | tf_op jit(solution)/shard_map/attend/pallas_call | solution.py:496
  203.6 0.0 copy-start.3
  203.6 0.7 copy-done.3
  204.3 42.2 %all_columns_1.3 = bf16[1024,2048]{1,0:T(8,128)(2,1)} custom-call(bf16[1024,128]{1,0:T(8,128)(2,1)} %copy-done.3), custom_call_target="tpu_custom_call" | custom-call | tf_op jit(solution)/shard_map/all_columns_1/pallas_call | solution.py:201
  246.5 4.2 %fusion.1.last = bf16[1024,128]{1,0:T(8,128)(2,1)} fusion(bf16[1024,2048]{1,0:T(8,128)(2,1)} %all_columns_1.3, bf16[2,2048,128]{2,1,0:T(8,128)(2,1)S(1)} %copy-done.5, bf16[1024,2048]{1,0:T(8,128)(2,1)} %all_columns_2.1.x_ref.mid, s32[]{:T(128)S(6)} %select_n.8), kind=kOutput, calls=%fused_computation.5 | convolution fusion | flops 537264128 | bytes 5242884 | tf_op jit(solution)/shard_map/dot_general | solution.py:515
  250.7 11.0 %deliver.1 = bf16[2,128,1024]{2,1,0:T(8,128)(2,1)} custom-call(bf16[1024,2048]{1,0:T(8,128)(2,1)} %all_columns_2.1.x_ref.mid, bf16[1024,128]{1,0:T(8,128)(2,1)} %fusion.1.last), custom_call_target="tpu_custom_call" | custom-call | tf_op jit(solution)/shard_map/deliver/pallas_call | solution.py:443
  261.7 1.9 copy.7
  (1 shorter events, 0.0 us)
Async XLA Ops:
  0.0 95.2 %copy-start = (s32[2,8,8]{2,1,0:T(8,128)S(1)}, s32[2,8,8]{2,1,0:T(8,128)}, u32[]{:S(2)}) copy-start(s32[2,8,8]{2,1,0:T(8,128)} %param.9) | copy-start | bytes 1540
  95.2 2.2 copy-start.2
  105.9 0.7 copy-start.4
  106.6 41.7 %copy-start.5 = (bf16[2,2048,128]{2,1,0:T(8,128)(2,1)S(1)}, bf16[2,2048,128]{2,1,0:T(8,128)(2,1)}, u32[]{:S(2)}) copy-start(bf16[2,2048,128]{2,1,0:T(8,128)(2,1)} %get-tuple-element.12) | copy-start | bytes 3145732
  193.2 2.2 copy-start.1
  203.6 0.7 copy-start.3

commit v2 on v1

--- a/solution.py
+++ b/solution.py
@@ -111,6 +111,7 @@
     return jnp.stack([first, second])[None]
 
 
+PIECES = 4
 MESH_ID = pl.DeviceIdType.MESH
 ANY = pl.BlockSpec(memory_space=pl.ANY)
 
@@ -158,9 +159,10 @@
 def columns_kernel(slot, own, out, local_sem, z_send, z_recv, y_send, y_recv, b_send, b_recv):
     core, x, y, z = place()
     wide = own.shape[1]
-
-    def region(c, yy, zz):
-        return out.at[:, pl.ds(pl.multiple_of(slot(c, yy, zz) * wide, wide), wide)]
+    rows = own.shape[0] // PIECES
+
+    def region(c, yy, zz, p):
+        return out.at[pl.ds(p * rows, rows), pl.ds(pl.multiple_of(slot(c, yy, zz) * wide, wide), wide)]
 
     far = [dev(core, x, y, z_apart(z, d)) for d in (1, 2, 3)]
     beside, sibling = dev(core, x, 1 - y, z), dev(1 - core, x, y, z)
@@ -172,25 +174,30 @@
         copy.start()
         sent.append(copy)
 
-    mine = region(core, y, z)
-    send(own, mine, y_send.at[0], y_recv.at[0], beside)
-    for d in (3, 2, 1):
-        send(own, mine, z_send.at[d - 1], z_recv.at[d - 1], far[d - 1])
-    send(own, mine, b_send.at[0], b_recv.at[0], sibling)
-    keep = pltpu.make_async_copy(own, mine, local_sem)
+    for p in range(PIECES):
+        mine, spot = own.at[pl.ds(p * rows, rows), :], region(core, y, z, p)
+        for d in (1, 2, 3):
+            send(mine, spot, z_send.at[p, d - 1], z_recv.at[p, d - 1], far[d - 1])
+        send(mine, spot, y_send.at[p, 0], y_recv.at[p, 0], beside)
+        send(mine, spot, b_send.at[p, 0], b_recv.at[p, 0], sibling)
+    keep = pltpu.make_async_copy(own, out.at[:, pl.ds(pl.multiple_of(slot(core, y, z) * wide, wide), wide)], local_sem)
     keep.start()
-    for d in (1, 2, 3):
-        got = region(core, y, z_apart(z, d))
-        remote(own, got, z_send.at[d - 1], z_recv.at[d - 1], sibling).wait_recv()
-        send(got, got, y_send.at[d], y_recv.at[d], beside)
-        send(got, got, b_send.at[d], b_recv.at[d], sibling)
-    for d in range(4):
-        got = region(core, 1 - y, z_apart(z, d))
-        remote(own, got, y_send.at[d], y_recv.at[d], sibling).wait_recv()
-        send(got, got, b_send.at[4 + d], b_recv.at[4 + d], sibling)
-    for d in range(8):
-        got = region(1 - core, y if d < 4 else 1 - y, z_apart(z, d % 4))
-        remote(own, got, b_send.at[d], b_recv.at[d], sibling).wait_recv()
+    like = own.at[pl.ds(0, rows), :]
+    for p in range(PIECES):
+        for d in (1, 2, 3):
+            got = region(core, y, z_apart(z, d), p)
+            remote(like, got, z_send.at[p, d - 1], z_recv.at[p, d - 1], sibling).wait_recv()
+            send(got, got, y_send.at[p, d], y_recv.at[p, d], beside)
+            send(got, got, b_send.at[p, d], b_recv.at[p, d], sibling)
+    for p in range(PIECES):
+        for d in range(4):
+            got = region(core, 1 - y, z_apart(z, d), p)
+            remote(like, got, y_send.at[p, d], y_recv.at[p, d], sibling).wait_recv()
+            send(got, got, b_send.at[p, 4 + d], b_recv.at[p, 4 + d], sibling)
+    for p in range(PIECES):
+        for d in range(8):
+            got = region(1 - core, y if d < 4 else 1 - y, z_apart(z, d % 4), p)
+            remote(like, got, b_send.at[p, d], b_recv.at[p, d], sibling).wait_recv()
     for copy in sent:
         copy.wait_send()
     keep.wait()
@@ -198,12 +205,13 @@
 
 def all_columns(own, slot, ident):
     dma = pltpu.SemaphoreType.DMA
+    counts = [(PIECES, c) for c in (3, 3, 4, 4, 8, 8)]
     return pl.pallas_call(
         functools.partial(columns_kernel, slot),
         out_shape=jax.ShapeDtypeStruct((own.shape[0], own.shape[1] * 16), own.dtype),
         in_specs=[ANY],
         out_specs=ANY,
-        scratch_shapes=[dma(()), dma((3,)), dma((3,)), dma((4,)), dma((4,)), dma((8,)), dma((8,))],
+        scratch_shapes=[dma(())] + [dma(c) for c in counts],
         compiler_params=pltpu.CompilerParams(collective_id=ident, has_side_effects=True),
         name="all_columns_%d" % ident,
     )(own)
@@ -251,13 +259,20 @@
     spot = region(core, x, y, z)
     send(other, spot, x_send, x_recv, across)
     send(mine, spot, y_send.at[0], y_recv.at[0], beside)
-    for d in (3, 2, 1):
+    for d in (1, 2, 3):
         send(mine, spot, z_send.at[d - 1], z_recv.at[d - 1], dev(core, x, y, far[d - 1]))
     send(mine, spot, b_send.at[0], b_recv.at[0], sibling)
     keep(mine, spot, l_sem.at[0])
     send(gain, gains.at[core], g_send, g_recv, sibling)
     keep(gain, gains.at[core], l_sem.at[1])
 
+    far_x = region(core, 1 - x, y, z)
+    remote(mine, far_x, x_send, x_recv, sibling).wait_recv()
+    send(far_x, far_x, y_send.at[4], y_recv.at[4], beside)
+    for d in (1, 2, 3):
+        send(far_x, far_x, z_send.at[2 + d], z_recv.at[2 + d], dev(core, x, y, far[d - 1]))
+    send(far_x, far_x, b_send.at[8], b_recv.at[8], sibling)
+
     def head_columns(zz, c):
         return w_qkv.at[0, :, :, pl.ds(pl.multiple_of((zz * 2 + c) * HD, HD), HD)]
 
@@ -265,7 +280,7 @@
         return wq.at[c, :, pl.ds(pl.multiple_of((zz * 2 + xx) * depth, depth), depth), :]
 
     own_rows = depth_rows(core, x, z)
-    for d in (0, 3, 2, 1):
+    for d in range(4):
         zz = z_apart(z, d)
         for other_core in range(2):
             target = 1 - core if other_core else core
@@ -276,6 +291,13 @@
                 at = 2 * d + other_core
                 send(head_columns(zz, target), own_rows, q_send.at[at], q_recv.at[at], dev(target, x, y, zz))
 
+    for k in range(2):
+        xx = 1 - x if k else x
+        for d in (1, 2, 3):
+            got = region(core, xx, y, far[d - 1])
+            remote(mine, got, x_send, z_recv.at[3 * k + d - 1], sibling).wait_recv()
+            send(got, got, y_send.at[4 * k + d], y_recv.at[4 * k + d], beside)
+            send(got, got, b_send.at[8 * k + d], b_recv.at[8 * k + d], sibling)
     half_rows = w_out.shape[1]
     to = wo.at[core, pl.ds(pl.multiple_of(y * half_rows, half_rows), half_rows), :]
     projections = []
@@ -293,19 +315,6 @@
                 copy.start()
             projections.append(copy)
 
-    far_x = region(core, 1 - x, y, z)
-    remote(mine, far_x, x_send, x_recv, sibling).wait_recv()
-    send(far_x, far_x, y_send.at[4], y_recv.at[4], beside)
-    for d in (3, 2, 1):
-        send(far_x, far_x, z_send.at[2 + d], z_recv.at[2 + d], dev(core, x, y, far[d - 1]))
-    send(far_x, far_x, b_send.at[8], b_recv.at[8], sibling)
-    for k in range(2):
-        xx = 1 - x if k else x
-        for d in (1, 2, 3):
-            got = region(core, xx, y, far[d - 1])
-            remote(mine, got, x_send, z_recv.at[3 * k + d - 1], sibling).wait_recv()
-            send(got, got, y_send.at[4 * k + d], y_recv.at[4 * k + d], beside)
-            send(got, got, b_send.at[8 * k + d], b_recv.at[8 * k + d], sibling)
     for d in range(4):
         for other_core in range(2):
             at = 2 * d + other_core
@@ -453,55 +462,60 @@
 
 def attend_kernel(x_ref, gain_ref, w_ref, flags, out_ref, q_ref, k_ref, v_ref):
     count = flags.shape[0]
-    rows = x_ref.shape[0] // count
-    step = 2 * rows
+    step = x_ref.shape[0]
+    rows = q_ref.shape[0] // count
     width = count.bit_length() - 1
     bits = [width - 1, width // 2, 0]
-
-    def project(at, _):
-        span = pl.ds(pl.multiple_of(at * step, step), step)
-        xf = x_ref[span, :].astype(jnp.float32)
-        inv = lax.rsqrt(jnp.mean(xf * xf, axis=-1, keepdims=True) + EPS)
-        normed = (xf * inv * gain_ref[...]).astype(jnp.bfloat16)
-        for part, ref in enumerate((q_ref, k_ref, v_ref)):
-            ref[span, :] = jnp.dot(normed, w_ref[part], preferred_element_type=jnp.float32).astype(jnp.bfloat16)
-        return 0
-
-    lax.fori_loop(0, x_ref.shape[0] // step, project, 0)
-    for block in range(count):
-        seen = [block] + [block ^ (1 << bit) for bit in bits]
-        span = slice(block * rows, (block + 1) * rows)
-        query = q_ref[span, :]
-        scores = []
-        for other in seen:
-            key = k_ref[other * rows : (other + 1) * rows, :]
-            dots = lax.dot_general(query, key, (((1,), (1,)), ((), ())), preferred_element_type=jnp.float32)
-            scores.append(jnp.where(flags[block, other] > 0, dots * (1.0 / HD**0.5), NEG))
-        top = functools.reduce(jnp.maximum, [jnp.max(s, axis=-1, keepdims=True) for s in scores])
-        total = jnp.zeros_like(top)
-        summed = jnp.zeros((rows, HD), jnp.float32)
-        for other, s in zip(seen, scores):
-            expo = jnp.where(flags[block, other] > 0, jnp.exp(s - top), 0.0)
-            total = total + jnp.sum(expo, axis=-1, keepdims=True)
-            summed = summed + jnp.dot(
-                expo.astype(jnp.bfloat16), v_ref[other * rows : (other + 1) * rows, :],
-                preferred_element_type=jnp.float32,
-            )
-        out_ref[span, :] = (summed / total).astype(jnp.bfloat16)
-
-
-def attend(x, gain_row, w, flags):
-    vmem = pl.BlockSpec(memory_space=pltpu.VMEM)
-    rows = x.shape[0]
+    at = pl.program_id(0)
+    here = pl.ds(pl.multiple_of(at * step, step), step)
+    xf = x_ref[...].astype(jnp.float32)
+    inv = lax.rsqrt(jnp.mean(xf * xf, axis=-1, keepdims=True) + EPS)
+    normed = (xf * inv * gain_ref[0]).astype(jnp.bfloat16)
+    for part, ref in enumerate((q_ref, k_ref, v_ref)):
+        ref[here, :] = jnp.dot(normed, w_ref[0, part], preferred_element_type=jnp.float32).astype(jnp.bfloat16)
+
+    @pl.when(at == pl.num_programs(0) - 1)
+    def _():
+        for block in range(count):
+            seen = [block] + [block ^ (1 << bit) for bit in bits]
+            span = slice(block * rows, (block + 1) * rows)
+            query = q_ref[span, :]
+            scores = []
+            for other in seen:
+                key = k_ref[other * rows : (other + 1) * rows, :]
+                dots = lax.dot_general(query, key, (((1,), (1,)), ((), ())), preferred_element_type=jnp.float32)
+                scores.append(jnp.where(flags[block, other] > 0, dots * (1.0 / HD**0.5), NEG))
+            top = functools.reduce(jnp.maximum, [jnp.max(s, axis=-1, keepdims=True) for s in scores])
+            total = jnp.zeros_like(top)
+            summed = jnp.zeros((rows, HD), jnp.float32)
+            for other, s in zip(seen, scores):
+                expo = jnp.where(flags[block, other] > 0, jnp.exp(s - top), 0.0)
+                total = total + jnp.sum(expo, axis=-1, keepdims=True)
+                summed = summed + jnp.dot(
+                    expo.astype(jnp.bfloat16), v_ref[other * rows : (other + 1) * rows, :],
+                    preferred_element_type=jnp.float32,
+                )
+            out_ref[span, :] = (summed / total).astype(jnp.bfloat16)
+
+
+def attend(x, gains, w, flags, s):
+    rows, wide = x.shape
+    step = rows // 4
     return pl.pallas_call(
         attend_kernel,
+        grid=(4,),
         out_shape=jax.ShapeDtypeStruct((rows, HD), jnp.bfloat16),
-        in_specs=[vmem, vmem, vmem, pl.BlockSpec(memory_space=pltpu.SMEM)],
-        out_specs=vmem,
+        in_specs=[
+            pl.BlockSpec((step, wide), lambda i: (i, 0)),
+            pl.BlockSpec((1, 1, wide), lambda i: (s, 0, 0)),
+            pl.BlockSpec((1, 3, wide, HD), lambda i: (s, 0, 0, 0)),
+            pl.BlockSpec(memory_space=pltpu.SMEM),
+        ],
+        out_specs=pl.BlockSpec((rows, HD), lambda i: (0, 0)),
         scratch_shapes=[pltpu.VMEM((rows, HD), jnp.bfloat16)] * 3,
         compiler_params=pltpu.CompilerParams(vmem_limit_bytes=40 * 2**20),
         name="attend",
-    )(x, gain_row, w, flags)
+    )(x, gains, w, flags)
 
 
 def local_planes(feats, gain, w_qkv, w_out, block_mask):
@@ -511,7 +525,7 @@
     column = column_slot(core, y, z) * HD
 
     def layer(x, s):
-        attended = all_columns(attend(x, gains[s], wq[s], flags), head_slot, 1)
+        attended = all_columns(attend(x, gains, wq, flags, s), head_slot, 1)
         projected = jnp.dot(attended, wo[s], preferred_element_type=jnp.float32)
         residual = lax.dynamic_slice_in_dim(x, column, HD, axis=1)
         return (residual.astype(jnp.float32) + projected).astype(jnp.bfloat16)

time: 267 us -> 222 us (0.83)
  Pallas kernels: 245 us -> 199 us
    pallas_call x1, Pallas kernels: 92.3 us -> 68.6 us  [spread(): pl.pallas_call(spread_kernel, out_shape=(jax.ShapeDtypeStruct((rows, wide...]
    pallas_call x3, Pallas kernels: 125 us -> 103 us  [all_columns(): pl.pallas_call(functools.partial(columns_kernel, slot), out_shape=jax.Sha...]
    unnamed x13 -> x21, local copies, waits for them, and re-layouts: 7.63 us -> 10.9 us
    squeeze x2 -> x0, local copies, waits for them, and re-layouts: 2.8 us -> none  [layer(): attended = all_columns(attend(x, gains[s], wq[s], flags), head_slot, 1)]
where the time goes in v2:
time: 222 us; the launch traced here: 219 us
  Pallas kernels  199 us (90%)
  local copies, waits for them, and re-layouts  10.9 us (5%)
  matrix products  8.68 us (4%)
    pallas_call x3, Pallas kernels, all_columns(): pl.pallas_call(functools.partial(columns_kernel, slot), out_shape=jax.Sha...  103 us
    pallas_call x1, Pallas kernels, spread(): pl.pallas_call(spread_kernel, out_shape=(jax.ShapeDtypeStruct((rows, wide...  68.6 us
    pallas_call x2, Pallas kernels, attend(): pl.pallas_call(attend_kernel, grid=(4,), out_shape=jax.ShapeDtypeStruct((...  16.6 us
    pallas_call x1, Pallas kernels, deliver(): pl.pallas_call(deliver_kernel, out_shape=jax.ShapeDtypeStruct((2, mid.sha...  11.5 us
    unnamed x21, local copies, waits for them, and re-layouts  10.9 us
    dot_general x2, matrix products, layer(): projected = jnp.dot(attended, wo[s], preferred_element_type=jnp.float32)  8.68 us

profile of v2, /device:TPU:25, one launch (start us, length us, event | category | flops | bytes accessed | tf_op | source)
XLA Modules:
  0.0 219.2 jit_solution(17825723290933285373)
XLA Ops:
  0.0 0.0 copy-start
  0.0 0.7 copy-done
  0.7 68.6 %spread.1 = (bf16[1024,2048]{1,0:T(8,128)(2,1)}, f32[2,1,2048]{2,1,0:T(1,128)}, bf16[2,3,2048,128]{3,2,1,0:T(8,128)(2,1)}, bf16[2,2048,128]{2,1,0:T(8,128)(2,1)}) custom-call(bf16[2,128,1024]{2,1,0:T(8,128)(2,1)} %feats.1, f32[1,2048]{1,0:T(1,128)} %gain.1, bf16[1,3,256,1024]{3,2,1,0:T(8,128)(2,1)} %w_qkv.1, bf16[1,1024,256]{2,1,0:T(8,128)(2,1)} %w_out.1), custom_call_target="tpu_custom_call" | custom-call | tf_op jit(solution)/shard_map/spread/pallas_call | solution.py:360
  69.3 0.0 copy-start.2
  69.3 1.9 copy-done.2
  71.2 0.0 copy-start.4
  71.2 2.2 copy-done.4
  73.4 0.0 copy-start.7
  73.4 0.7 copy-done.7
  74.1 8.3 %attend.2.own = bf16[1024,128]{1,0:T(8,128)(2,1)S(1)} custom-call(bf16[1024,2048]{1,0:T(8,128)(2,1)S(1)} %copy-done.4, f32[2,1,2048]{2,1,0:T(1,128)S(1)} %copy-done.7, bf16[2,3,2048,128]{3,2,1,0:T(8,128)(2,1)S(1)} %copy-done.2, s32[8,8]{1,0:T(8,128)S(1)} %dynamic-slice_bitcast_fusion.flags), custom_call_target="tpu_custom_call" | custom-call | tf_op jit(solution)/shard_map/attend/pallas_call | solution.py:504
  82.4 0.0 copy-start.6
  82.4 0.7 copy-done.6
  83.1 34.9 %all_columns_1.2 = bf16[1024,2048]{1,0:T(8,128)(2,1)} custom-call(bf16[1024,128]{1,0:T(8,128)(2,1)} %copy-done.6), custom_call_target="tpu_custom_call" | custom-call | tf_op jit(solution)/shard_map/all_columns_1/pallas_call | solution.py:209
  118.0 0.0 copy-start.3
  118.0 0.0 copy-start.8
  118.0 4.5 %fusion.own = bf16[1024,128]{1,0:T(8,128)(2,1)} fusion(bf16[1024,2048]{1,0:T(8,128)(2,1)} %all_columns_1.2, bf16[2,2048,128]{2,1,0:T(8,128)(2,1)} %get-tuple-element.12, bf16[1024,2048]{1,0:T(8,128)(2,1)} %get-tuple-element.9.x_ref, s32[]{:T(128)S(6)} %select_n.8), kind=kOutput, calls=%fused_computation.2 | convolution fusion | flops 537264128 | bytes 5242884 | tf_op jit(solution)/shard_map/dot_general | solution.py:529
  122.5 35.1 %all_columns_2.1.x_ref.mid = bf16[1024,2048]{1,0:T(8,128)(2,1)} custom-call(bf16[1024,128]{1,0:T(8,128)(2,1)} %fusion.own), custom_call_target="tpu_custom_call" | custom-call | tf_op jit(solution)/shard_map/all_columns_2/pallas_call | solution.py:209
  157.6 0.0 copy-done.3
  157.6 0.0 copy-done.8
  157.6 0.0 copy-start.1
  157.7 2.2 copy-done.1
  159.8 8.4 %attend.3.own = bf16[1024,128]{1,0:T(8,128)(2,1)S(1)} custom-call(bf16[1024,2048]{1,0:T(8,128)(2,1)S(1)} %copy-done.1, f32[2,1,2048]{2,1,0:T(1,128)S(1)} %copy-done.8, bf16[2,3,2048,128]{3,2,1,0:T(8,128)(2,1)S(1)} %copy-done.3, s32[8,8]{1,0:T(8,128)S(1)} %dynamic-slice_bitcast_fusion.flags), custom_call_target="tpu_custom_call" | custom-call | tf_op jit(solution)/shard_map/attend/pallas_call | solution.py:504
  168.2 0.0 copy-start.5
  168.2 0.7 copy-done.5
  168.9 0.0 copy-start.9
  168.9 32.7 %all_columns_1.3 = bf16[1024,2048]{1,0:T(8,128)(2,1)} custom-call(bf16[1024,128]{1,0:T(8,128)(2,1)} %copy-done.5), custom_call_target="tpu_custom_call" | custom-call | tf_op jit(solution)/shard_map/all_columns_1/pallas_call | solution.py:209
  201.7 0.0 copy-done.9
  201.7 4.2 %fusion.1.last = bf16[1024,128]{1,0:T(8,128)(2,1)} fusion(bf16[1024,2048]{1,0:T(8,128)(2,1)} %all_columns_1.3, bf16[2,2048,128]{2,1,0:T(8,128)(2,1)S(1)} %copy-done.9, bf16[1024,2048]{1,0:T(8,128)(2,1)} %all_columns_2.1.x_ref.mid, s32[]{:T(128)S(6)} %select_n.8), kind=kOutput, calls=%fused_computation.3 | convolution fusion | flops 537264128 | bytes 5242884 | tf_op jit(solution)/shard_map/dot_general | solution.py:529
  205.9 11.5 %deliver.1 = bf16[2,128,1024]{2,1,0:T(8,128)(2,1)} custom-call(bf16[1024,2048]{1,0:T(8,128)(2,1)} %all_columns_2.1.x_ref.mid, bf16[1024,128]{1,0:T(8,128)(2,1)} %fusion.1.last), custom_call_target="tpu_custom_call" | custom-call | tf_op jit(solution)/shard_map/deliver/pallas_call | solution.py:452
  217.4 1.9 copy.7
  (1 shorter events, 0.0 us)
Async XLA Ops:
  0.0 0.7 copy-start
  69.3 1.9 copy-start.2
  71.2 2.2 copy-start.4
  73.4 0.7 copy-start.7
  82.4 0.7 copy-start.6
  118.0 39.6 %copy-start.3 = (bf16[2,3,2048,128]{3,2,1,0:T(8,128)(2,1)S(1)}, bf16[2,3,2048,128]{3,2,1,0:T(8,128)(2,1)}, u32[]{:S(2)}) copy-start(bf16[2,3,2048,128]{3,2,1,0:T(8,128)(2,1)} %get-tuple-element.11.w_ref) | copy-start | bytes 9437188
  118.0 39.6 %copy-start.8 = (f32[2,1,2048]{2,1,0:T(1,128)S(1)}, f32[2,1,2048]{2,1,0:T(1,128)}, u32[]{:S(2)}) copy-start(f32[2,1,2048]{2,1,0:T(1,128)} %get-tuple-element.10.gain_ref) | copy-start | bytes 49156
  157.6 2.2 copy-start.1
  168.2 0.7 copy-start.5
  168.9 32.8 %copy-start.9 = (bf16[2,2048,128]{2,1,0:T(8,128)(2,1)S(1)}, bf16[2,2048,128]{2,1,0:T(8,128)(2,1)}, u32[]{:S(2)}) copy-start(bf16[2,2048,128]{2,1,0:T(8,128)(2,1)} %get-tuple-element.12) | copy-start | bytes 3145732

commit v3 on v2

--- a/solution.py
+++ b/solution.py
@@ -156,65 +156,140 @@
     return 4 * z + 2 * y + core
 
 
-def columns_kernel(slot, own, out, local_sem, z_send, z_recv, y_send, y_recv, b_send, b_recv):
-    core, x, y, z = place()
-    wide = own.shape[1]
-    rows = own.shape[0] // PIECES
-
-    def region(c, yy, zz, p):
-        return out.at[pl.ds(p * rows, rows), pl.ds(pl.multiple_of(slot(c, yy, zz) * wide, wide), wide)]
-
-    far = [dev(core, x, y, z_apart(z, d)) for d in (1, 2, 3)]
-    beside, sibling = dev(core, x, 1 - y, z), dev(1 - core, x, y, z)
-    greet(far + [beside, sibling])
-    sent = []
-
-    def send(src, dst, ssem, rsem, target):
+class Gather:
+    def __init__(self, slot, own, out, sems, sent):
+        self.slot, self.own, self.out, self.sent = slot, own, out, sent
+        self.local, self.zs, self.zr, self.ys, self.yr, self.bs, self.br = sems
+        self.at = place()
+        self.rows, self.wide = own.shape[0] // PIECES, own.shape[1]
+        core, x, y, z = self.at
+        self.far = [dev(core, x, y, z_apart(z, d)) for d in (1, 2, 3)]
+        self.beside, self.sibling = dev(core, x, 1 - y, z), dev(1 - core, x, y, z)
+
+    def peers(self):
+        return self.far + [self.beside, self.sibling]
+
+    def mine(self, p):
+        return self.own.at[pl.ds(p * self.rows, self.rows), :]
+
+    def region(self, c, yy, zz, p):
+        column = pl.multiple_of(self.slot(c, yy, zz) * self.wide, self.wide)
+        return self.out.at[pl.ds(p * self.rows, self.rows), pl.ds(column, self.wide)]
+
+    def send(self, src, dst, ssem, rsem, target):
         copy = remote(src, dst, ssem, rsem, target)
         copy.start()
-        sent.append(copy)
-
+        self.sent.append(copy.wait_send)
+
+    def await_recv(self, got, sem):
+        remote(self.mine(0), got, sem, sem, self.sibling).wait_recv()
+
+    def start(self, p):
+        core, x, y, z = self.at
+        mine, spot = self.mine(p), self.region(core, y, z, p)
+        for d in (1, 2, 3):
+            self.send(mine, spot, self.zs.at[p, d - 1], self.zr.at[p, d - 1], self.far[d - 1])
+        self.send(mine, spot, self.ys.at[p, 0], self.yr.at[p, 0], self.beside)
+        self.send(mine, spot, self.bs.at[p, 0], self.br.at[p, 0], self.sibling)
+        pltpu.make_async_copy(mine, spot, self.local.at[p]).start()
+
+    def along_z(self, p):
+        core, x, y, z = self.at
+        for d in (1, 2, 3):
+            got = self.region(core, y, z_apart(z, d), p)
+            self.await_recv(got, self.zr.at[p, d - 1])
+            self.send(got, got, self.ys.at[p, d], self.yr.at[p, d], self.beside)
+            self.send(got, got, self.bs.at[p, d], self.br.at[p, d], self.sibling)
+
+    def along_y(self, p):
+        core, x, y, z = self.at
+        for d in range(4):
+            got = self.region(core, 1 - y, z_apart(z, d), p)
+            self.await_recv(got, self.yr.at[p, d])
+            self.send(got, got, self.bs.at[p, 4 + d], self.br.at[p, 4 + d], self.sibling)
+
+    def whole(self, p):
+        core, x, y, z = self.at
+        for d in range(8):
+            got = self.region(1 - core, y if d < 4 else 1 - y, z_apart(z, d % 4), p)
+            self.await_recv(got, self.br.at[p, d])
+        pltpu.make_async_copy(self.mine(p), self.region(core, y, z, p), self.local.at[p]).wait()
+
+
+def gather_sems():
+    dma = pltpu.SemaphoreType.DMA
+    return [dma((PIECES,))] + [dma((PIECES, c)) for c in (3, 3, 4, 4, 8, 8)]
+
+
+def own_columns(array):
+    core, x, y, z = place()
+    return array.at[:, pl.ds(pl.multiple_of(column_slot(core, y, z) * HD, HD), HD)]
+
+
+def project_piece(all_ref, wo_ref, s, rest_ref, into_ref, p):
+    rows = all_ref.shape[0] // PIECES
+    span = slice(p * rows, (p + 1) * rows)
+    projected = jnp.dot(all_ref[span, :], wo_ref[s], preferred_element_type=jnp.float32)
+    into_ref[span, :] = (rest_ref[span, :].astype(jnp.float32) + projected).astype(jnp.bfloat16)
+
+
+def turn_kernel(
+    own, x, wo_ref, gain_ref, w_ref, flags, mid, out_ref,
+    all_ref, rest_ref, into_ref, q_ref, k_ref, v_ref, rest_sem, *sems,
+):
+    sent = []
+    heads = Gather(head_slot, own, all_ref, sems[:7], sent)
+    columns = Gather(column_slot, into_ref, mid, sems[7:], sent)
+    greet(heads.peers())
     for p in range(PIECES):
-        mine, spot = own.at[pl.ds(p * rows, rows), :], region(core, y, z, p)
-        for d in (1, 2, 3):
-            send(mine, spot, z_send.at[p, d - 1], z_recv.at[p, d - 1], far[d - 1])
-        send(mine, spot, y_send.at[p, 0], y_recv.at[p, 0], beside)
-        send(mine, spot, b_send.at[p, 0], b_recv.at[p, 0], sibling)
-    keep = pltpu.make_async_copy(own, out.at[:, pl.ds(pl.multiple_of(slot(core, y, z) * wide, wide), wide)], local_sem)
-    keep.start()
-    like = own.at[pl.ds(0, rows), :]
-    for p in range(PIECES):
-        for d in (1, 2, 3):
-            got = region(core, y, z_apart(z, d), p)
-            remote(like, got, z_send.at[p, d - 1], z_recv.at[p, d - 1], sibling).wait_recv()
-            send(got, got, y_send.at[p, d], y_recv.at[p, d], beside)
-            send(got, got, b_send.at[p, d], b_recv.at[p, d], sibling)
-    for p in range(PIECES):
-        for d in range(4):
-            got = region(core, 1 - y, z_apart(z, d), p)
-            remote(like, got, y_send.at[p, d], y_recv.at[p, d], sibling).wait_recv()
-            send(got, got, b_send.at[p, 4 + d], b_recv.at[p, 4 + d], sibling)
-    for p in range(PIECES):
-        for d in range(8):
-            got = region(1 - core, y if d < 4 else 1 - y, z_apart(z, d % 4), p)
-            remote(like, got, b_send.at[p, d], b_recv.at[p, d], sibling).wait_recv()
-    for copy in sent:
-        copy.wait_send()
-    keep.wait()
-
-
-def all_columns(own, slot, ident):
+        heads.start(p)
+    rest = pltpu.make_async_copy(own_columns(x), rest_ref, rest_sem)
+    rest.start()
+    rest.wait()
+    rows = mid.shape[0] // PIECES
+    for step in range(2 * PIECES + 2):
+        for stage in range(3):
+            part = step - stage
+            if part < 0 or part >= 2 * PIECES:
+                continue
+            gather, p = (heads, part) if part < PIECES else (columns, part - PIECES)
+            if stage == 0:
+                gather.along_z(p)
+            elif stage == 1:
+                gather.along_y(p)
+            else:
+                gather.whole(p)
+                if gather is heads:
+                    project_piece(all_ref, wo_ref, 0, rest_ref, into_ref, p)
+                    columns.start(p)
+                else:
+                    span = pl.ds(p * rows, rows)
+                    project_rows(
+                        mid[span, :].astype(jnp.float32), gain_ref[1], lambda part: w_ref[1, part],
+                        (q_ref, k_ref, v_ref), span,
+                    )
+    attend_blocks(q_ref, k_ref, v_ref, flags, out_ref)
+    for wait in sent:
+        wait()
+
+
+def turn(own, x, wo, gains, w, flags):
     dma = pltpu.SemaphoreType.DMA
-    counts = [(PIECES, c) for c in (3, 3, 4, 4, 8, 8)]
+    vmem = pl.BlockSpec(memory_space=pltpu.VMEM)
+    rows, wide = x.shape
+    narrow = pltpu.VMEM((rows, HD), jnp.bfloat16)
     return pl.pallas_call(
-        functools.partial(columns_kernel, slot),
-        out_shape=jax.ShapeDtypeStruct((own.shape[0], own.shape[1] * 16), own.dtype),
-        in_specs=[ANY],
-        out_specs=ANY,
-        scratch_shapes=[dma(())] + [dma(c) for c in counts],
-        compiler_params=pltpu.CompilerParams(collective_id=ident, has_side_effects=True),
-        name="all_columns_%d" % ident,
-    )(own)
+        turn_kernel,
+        out_shape=(jax.ShapeDtypeStruct((rows, wide), x.dtype), jax.ShapeDtypeStruct((rows, HD), x.dtype)),
+        in_specs=[ANY, ANY, vmem, vmem, vmem, pl.BlockSpec(memory_space=pltpu.SMEM)],
+        out_specs=(vmem, vmem),
+        scratch_shapes=[pltpu.VMEM((rows, wide), jnp.bfloat16)] + [narrow] * 5 + [dma(())]
+        + gather_sems() + gather_sems(),
+        compiler_params=pltpu.CompilerParams(
+            collective_id=1, has_side_effects=True, vmem_limit_bytes=48 * 2**20
+        ),
+        name="turn",
+    )(own, x, wo, gains, w, flags)
 
 
 def spread_kernel(
@@ -374,7 +449,12 @@
     )(feats, gain, w_qkv, w_out)
 
 
-def deliver_kernel(mid, last, out, l_sem, m_send, m_recv, a_send, a_recv):
+def finish_kernel(
+    own, mid, wo_ref, out,
+    all_ref, rest_ref, last, rest_sem, l_sem, m_send, m_recv, a_send, a_recv, *sems,
+):
+    sent = []
+    heads = Gather(head_slot, own, all_ref, sems, sent)
     core, x, y, z = place()
     node = z * 2 + x
     rows, wide = out.shape[1], out.shape[2]
@@ -388,6 +468,9 @@
     def signal(peer):
         pl.semaphore_signal(barrier, inc=1, device_id=peer, device_id_type=MESH_ID)
 
+    for peer in heads.peers():
+        signal(peer)
+
     @pl.when(first)
     def _():
         signal(dev(0, 1 - x, y, z))
@@ -400,7 +483,12 @@
         def _():
             signal(dev(cc, xx, yy, 2 * y + zl))
 
-    pl.semaphore_wait(barrier, 8 - to_self.astype(jnp.int32) + first.astype(jnp.int32))
+    pl.semaphore_wait(barrier, 13 - to_self.astype(jnp.int32) + first.astype(jnp.int32))
+
+    for p in range(PIECES):
+        heads.start(p)
+    rest = pltpu.make_async_copy(own_columns(mid), rest_ref, rest_sem)
+    rest.start()
 
     def mid_rows(n):
         return mid.at[
@@ -419,13 +507,24 @@
     spot = out.at[x, :, pl.ds(pl.multiple_of(slot * piece, piece), piece)]
     index = 8 * z_low + 4 * x + 2 * y + core
     copies = []
-    for n in range(8):
-        src = last.at[pl.ds(n * rows, rows), :]
-        copy = remote(src, spot, a_send.at[n], a_recv.at[index], dev(1, n % 2, to_y, n // 2))
-        own = to_self & (node == n)
-        pl.when(jnp.logical_not(own))(copy.start)
-        pl.when(own)(pltpu.make_async_copy(src, spot, a_recv.at[index]).start)
-        copies.append((copy, own))
+    rest.wait()
+    for step in range(PIECES + 2):
+        if step < PIECES:
+            heads.along_z(step)
+        if 0 <= step - 1 < PIECES:
+            heads.along_y(step - 1)
+        p = step - 2
+        if p < 0:
+            continue
+        heads.whole(p)
+        project_piece(all_ref, wo_ref, 1, rest_ref, last, p)
+        for n in range(8 // PIECES * p, 8 // PIECES * (p + 1)):
+            src = last.at[pl.ds(n * rows, rows), :]
+            copy = remote(src, spot, a_send.at[n], a_recv.at[index], dev(1, n % 2, to_y, n // 2))
+            mine = to_self & (node == n)
+            pl.when(jnp.logical_not(mine))(copy.start)
+            pl.when(mine)(pltpu.make_async_copy(src, spot, a_recv.at[index]).start)
+            copies.append((copy, mine))
 
     @pl.when(first)
     def _():
@@ -443,59 +542,75 @@
                 dev(0, x, y, z),
             ).wait_recv()
 
-    for copy, own in copies:
-        pl.when(jnp.logical_not(own))(copy.wait_send)
-
-
-def deliver(mid, last):
+    for copy, mine in copies:
+        pl.when(jnp.logical_not(mine))(copy.wait_send)
+    for wait in sent:
+        wait()
+
+
+def finish_layers(own, mid, wo):
     dma = pltpu.SemaphoreType.DMA
+    rows, wide = mid.shape
+    narrow = pltpu.VMEM((rows, HD), jnp.bfloat16)
     return pl.pallas_call(
-        deliver_kernel,
-        out_shape=jax.ShapeDtypeStruct((2, mid.shape[0] // 8, mid.shape[1] // 2), mid.dtype),
-        in_specs=[ANY] * 2,
+        finish_kernel,
+        out_shape=jax.ShapeDtypeStruct((2, rows // 8, wide // 2), mid.dtype),
+        in_specs=[ANY, ANY, pl.BlockSpec(memory_space=pltpu.VMEM)],
         out_specs=ANY,
-        scratch_shapes=[dma(()), dma(()), dma(()), dma((8,)), dma((16,))],
-        compiler_params=pltpu.CompilerParams(collective_id=3, has_side_effects=True),
-        name="deliver",
-    )(mid, last)
-
-
-def attend_kernel(x_ref, gain_ref, w_ref, flags, out_ref, q_ref, k_ref, v_ref):
+        scratch_shapes=[pltpu.VMEM((rows, wide), jnp.bfloat16), narrow, narrow]
+        + [dma(()), dma(()), dma(()), dma(()), dma((8,)), dma((16,))] + gather_sems(),
+        compiler_params=pltpu.CompilerParams(
+            collective_id=3, has_side_effects=True, vmem_limit_bytes=40 * 2**20
+        ),
+        name="finish",
+    )(own, mid, wo)
+
+
+def project_rows(xf, gain_row, w_part, refs, here):
+    inv = lax.rsqrt(jnp.mean(xf * xf, axis=-1, keepdims=True) + EPS)
+    normed = (xf * inv * gain_row).astype(jnp.bfloat16)
+    for part, ref in enumerate(refs):
+        ref[here, :] = jnp.dot(normed, w_part(part), preferred_element_type=jnp.float32).astype(jnp.bfloat16)
+
+
+def attend_blocks(q_ref, k_ref, v_ref, flags, out_ref):
     count = flags.shape[0]
-    step = x_ref.shape[0]
     rows = q_ref.shape[0] // count
     width = count.bit_length() - 1
     bits = [width - 1, width // 2, 0]
+    for block in range(count):
+        seen = [block] + [block ^ (1 << bit) for bit in bits]
+        span = slice(block * rows, (block + 1) * rows)
+        query = q_ref[span, :]
+        scores = []
+        for other in seen:
+            key = k_ref[other * rows : (other + 1) * rows, :]
+            dots = lax.dot_general(query, key, (((1,), (1,)), ((), ())), preferred_element_type=jnp.float32)
+            scores.append(jnp.where(flags[block, other] > 0, dots * (1.0 / HD**0.5), NEG))
+        top = functools.reduce(jnp.maximum, [jnp.max(s, axis=-1, keepdims=True) for s in scores])
+        total = jnp.zeros_like(top)
+        summed = jnp.zeros((rows, HD), jnp.float32)
+        for other, s in zip(seen, scores):
+            expo = jnp.where(flags[block, other] > 0, jnp.exp(s - top), 0.0)
+            total = total + jnp.sum(expo, axis=-1, keepdims=True)
+            summed = summed + jnp.dot(
+                expo.astype(jnp.bfloat16), v_ref[other * rows : (other + 1) * rows, :],
+                preferred_element_type=jnp.float32,
+            )
+        out_ref[span, :] = (summed / total).astype(jnp.bfloat16)
+
+
+def attend_kernel(x_ref, gain_ref, w_ref, flags, out_ref, q_ref, k_ref, v_ref):
+    step = x_ref.shape[0]
     at = pl.program_id(0)
     here = pl.ds(pl.multiple_of(at * step, step), step)
-    xf = x_ref[...].astype(jnp.float32)
-    inv = lax.rsqrt(jnp.mean(xf * xf, axis=-1, keepdims=True) + EPS)
-    normed = (xf * inv * gain_ref[0]).astype(jnp.bfloat16)
-    for part, ref in enumerate((q_ref, k_ref, v_ref)):
-        ref[here, :] = jnp.dot(normed, w_ref[0, part], preferred_element_type=jnp.float32).astype(jnp.bfloat16)
+    project_rows(
+        x_ref[...].astype(jnp.float32), gain_ref[0], lambda part: w_ref[0, part], (q_ref, k_ref, v_ref), here
+    )
 
     @pl.when(at == pl.num_programs(0) - 1)
     def _():
-        for block in range(count):
-            seen = [block] + [block ^ (1 << bit) for bit in bits]
-            span = slice(block * rows, (block + 1) * rows)
-            query = q_ref[span, :]
-            scores = []
-            for other in seen:
-                key = k_ref[other * rows : (other + 1) * rows, :]
-                dots = lax.dot_general(query, key, (((1,), (1,)), ((), ())), preferred_element_type=jnp.float32)
-                scores.append(jnp.where(flags[block, other] > 0, dots * (1.0 / HD**0.5), NEG))
-            top = functools.reduce(jnp.maximum, [jnp.max(s, axis=-1, keepdims=True) for s in scores])
-            total = jnp.zeros_like(top)
-            summed = jnp.zeros((rows, HD), jnp.float32)
-            for other, s in zip(seen, scores):
-                expo = jnp.where(flags[block, other] > 0, jnp.exp(s - top), 0.0)
-                total = total + jnp.sum(expo, axis=-1, keepdims=True)
-                summed = summed + jnp.dot(
-                    expo.astype(jnp.bfloat16), v_ref[other * rows : (other + 1) * rows, :],
-                    preferred_element_type=jnp.float32,
-                )
-            out_ref[span, :] = (summed / total).astype(jnp.bfloat16)
+        attend_blocks(q_ref, k_ref, v_ref, flags, out_ref)
 
 
 def attend(x, gains, w, flags, s):
@@ -522,16 +637,8 @@
     core, micro, y, z = place()
     flags = lax.dynamic_index_in_dim(block_mask, micro, 0, keepdims=False)
     whole, gains, wq, wo = spread(feats, gain, w_qkv, w_out)
-    column = column_slot(core, y, z) * HD
-
-    def layer(x, s):
-        attended = all_columns(attend(x, gains, wq, flags, s), head_slot, 1)
-        projected = jnp.dot(attended, wo[s], preferred_element_type=jnp.float32)
-        residual = lax.dynamic_slice_in_dim(x, column, HD, axis=1)
-        return (residual.astype(jnp.float32) + projected).astype(jnp.bfloat16)
-
-    mid = all_columns(layer(whole, 0), column_slot, 2)
-    return deliver(mid, layer(mid, 1))[None]
+    mid, attended = turn(attend(whole, gains, wq, flags, 0), whole, wo, gains, wq, flags)
+    return finish_layers(attended, mid, wo)[None]
 
 
 def solution(mesh):

time: 222 us -> 194 us (0.87)
  Pallas kernels: 199 us -> 185 us
  matrix products: 8.68 us -> 0 us
  local copies, waits for them, and re-layouts: 10.9 us -> 8.47 us
    dot_general x2 -> x0, matrix products: 8.68 us -> none  [layer(): projected = jnp.dot(attended, wo[s], preferred_element_type=jnp.float32)]
    pallas_call x2 -> x1, Pallas kernels: 16.6 us -> 8.4 us  [attend(): pl.pallas_call(attend_kernel, grid=(4,), out_shape=jax.ShapeDtypeStruct((...]
    pallas_call x4 -> x2, Pallas kernels: 114 us -> 108 us  [the longest x1 63.6 us: turn(): pl.pallas_call(turn_kernel, out_shape=(jax.ShapeDtypeStruct((rows, wide),...]
    unnamed x21 -> x17, local copies, waits for them, and re-layouts: 10.9 us -> 8.47 us
where the time goes in v3:
time: 194 us; the launch traced here: 193 us
  Pallas kernels  185 us (95%)
  local copies, waits for them, and re-layouts  8.47 us (4%)
    pallas_call x1, Pallas kernels, spread(): pl.pallas_call(spread_kernel, out_shape=(jax.ShapeDtypeStruct((rows, wide...  68.6 us
    pallas_call x1, Pallas kernels, turn(): pl.pallas_call(turn_kernel, out_shape=(jax.ShapeDtypeStruct((rows, wide),...  63.6 us
    pallas_call x1, Pallas kernels, finish_layers(): pl.pallas_call(finish_kernel, out_shape=jax.ShapeDtypeStruct((2, rows //...  44.1 us
    unnamed x17, local copies, waits for them, and re-layouts  8.47 us
    pallas_call x1, Pallas kernels, attend(): pl.pallas_call(attend_kernel, grid=(4,), out_shape=jax.ShapeDtypeStruct((...  8.4 us

profile of v3, /device:TPU:25, one launch (start us, length us, event | category | flops | bytes accessed | tf_op | source)
XLA Modules:
  0.0 193.3 jit_solution(14105355120647432314)
XLA Ops:
  0.0 0.0 copy-start
  0.0 0.7 copy-done
  0.7 68.6 %spread.1 = (bf16[1024,2048]{1,0:T(8,128)(2,1)}, f32[2,1,2048]{2,1,0:T(1,128)}, bf16[2,3,2048,128]{3,2,1,0:T(8,128)(2,1)}, bf16[2,2048,128]{2,1,0:T(8,128)(2,1)}) custom-call(bf16[2,128,1024]{2,1,0:T(8,128)(2,1)} %feats.1, f32[1,2048]{1,0:T(1,128)} %gain.1, bf16[1,3,256,1024]{3,2,1,0:T(8,128)(2,1)} %w_qkv.1, bf16[1,1024,256]{2,1,0:T(8,128)(2,1)} %w_out.1), custom_call_target="tpu_custom_call" | custom-call | tf_op jit(solution)/shard_map/spread/pallas_call | solution.py:435
  69.3 0.0 copy-start.1
  69.3 2.2 %copy-done.1 = bf16[1024,2048]{1,0:T(8,128)(2,1)S(1)} copy-done((bf16[1024,2048]{1,0:T(8,128)(2,1)S(1)}, bf16[1024,2048]{1,0:T(8,128)(2,1)}, u32[]{:S(2)}) %copy-start.1) | copy-done | bytes 4194328
  71.5 0.0 copy-start.2
  71.5 1.9 copy-done.2
  73.4 0.0 copy-start.6
  73.4 0.7 copy-done.6
  74.1 0.0 copy-start.3
  74.1 0.0 copy-start.5
  74.1 0.0 copy-start.7
  74.1 8.4 %attend.1.own = bf16[1024,128]{1,0:T(8,128)(2,1)S(1)} custom-call(bf16[1024,2048]{1,0:T(8,128)(2,1)S(1)} %copy-done.1, f32[2,1,2048]{2,1,0:T(1,128)S(1)} %copy-done.6, bf16[2,3,2048,128]{3,2,1,0:T(8,128)(2,1)S(1)} %copy-done.2, s32[8,8]{1,0:T(8,128)S(1)} %dynamic-slice_bitcast_fusion.flags), custom_call_target="tpu_custom_call" | custom-call | tf_op jit(solution)/shard_map/attend/pallas_call | solution.py:619
  82.5 0.0 copy-done.3
  82.6 0.0 copy-done.5
  82.6 0.0 copy-done.7
  82.6 63.6 %turn.1 = (bf16[1024,2048]{1,0:T(8,128)(2,1)}, bf16[1024,128]{1,0:T(8,128)(2,1)S(1)}) custom-call(bf16[1024,128]{1,0:T(8,128)(2,1)S(1)} %attend.1.own, bf16[1024,2048]{1,0:T(8,128)(2,1)} %get-tuple-element.11.x_ref.x, bf16[2,2048,128]{2,1,0:T(8,128)(2,1)S(1)} %copy-done.5, f32[2,1,2048]{2,1,0:T(1,128)S(1)} %copy-done.7, ...), custom_call_target="tpu_custom_call" | custom-call | tf_op jit(solution)/shard_map/turn/pallas_call | solution.py:281
  146.1 0.0 copy-start.4
  146.1 2.2 %copy-done.4 = bf16[1024,2048]{1,0:T(8,128)(2,1)S(1)} copy-done((bf16[1024,2048]{1,0:T(8,128)(2,1)S(1)}, bf16[1024,2048]{1,0:T(8,128)(2,1)}, u32[]{:S(2)}) %copy-start.4) | copy-done | bytes 4194328
  148.3 44.1 %finish.1 = bf16[2,128,1024]{2,1,0:T(8,128)(2,1)S(1)} custom-call(bf16[1024,128]{1,0:T(8,128)(2,1)S(1)} %get-tuple-element.15.own, bf16[1024,2048]{1,0:T(8,128)(2,1)S(1)} %copy-done.4, bf16[2,2048,128]{2,1,0:T(8,128)(2,1)S(1)} %copy-done.5), custom_call_target="tpu_custom_call" | custom-call | tf_op jit(solution)/shard_map/finish/pallas_call | solution.py:555
  192.5 0.8 copy.7
  (1 shorter events, 0.0 us)
Async XLA Ops:
  0.0 0.7 copy-start
  69.3 2.2 %copy-start.1 = (bf16[1024,2048]{1,0:T(8,128)(2,1)S(1)}, bf16[1024,2048]{1,0:T(8,128)(2,1)}, u32[]{:S(2)}) copy-start(bf16[1024,2048]{1,0:T(8,128)(2,1)} %get-tuple-element.11.x_ref.x) | copy-start | bytes 12582916
  71.5 1.9 copy-start.2
  73.4 0.7 copy-start.6
  74.1 8.4 %copy-start.3 = (bf16[2,3,2048,128]{3,2,1,0:T(8,128)(2,1)S(1)}, bf16[2,3,2048,128]{3,2,1,0:T(8,128)(2,1)}, u32[]{:S(2)}) copy-start(bf16[2,3,2048,128]{3,2,1,0:T(8,128)(2,1)} %get-tuple-element.13.w_ref) | copy-start | bytes 9437188
  74.1 8.4 %copy-start.5 = (bf16[2,2048,128]{2,1,0:T(8,128)(2,1)S(1)}, bf16[2,2048,128]{2,1,0:T(8,128)(2,1)}, u32[]{:S(2)}) copy-start(bf16[2,2048,128]{2,1,0:T(8,128)(2,1)} %get-tuple-element.14.wo_ref) | copy-start | bytes 3145732
  74.1 8.4 %copy-start.7 = (f32[2,1,2048]{2,1,0:T(1,128)S(1)}, f32[2,1,2048]{2,1,0:T(1,128)}, u32[]{:S(2)}) copy-start(f32[2,1,2048]{2,1,0:T(1,128)} %get-tuple-element.12.gain_ref) | copy-start | bytes 49156
  146.1 2.2 %copy-start.4 = (bf16[1024,2048]{1,0:T(8,128)(2,1)S(1)}, bf16[1024,2048]{1,0:T(8,128)(2,1)}, u32[]{:S(2)}) copy-start(bf16[1024,2048]{1,0:T(8,128)(2,1)} %get-tuple-element.16.mid) | copy-start | bytes 12582916

commit v4 on v3

--- a/solution.py
+++ b/solution.py
@@ -233,69 +233,11 @@
     into_ref[span, :] = (rest_ref[span, :].astype(jnp.float32) + projected).astype(jnp.bfloat16)
 
 
-def turn_kernel(
-    own, x, wo_ref, gain_ref, w_ref, flags, mid, out_ref,
-    all_ref, rest_ref, into_ref, q_ref, k_ref, v_ref, rest_sem, *sems,
-):
-    sent = []
-    heads = Gather(head_slot, own, all_ref, sems[:7], sent)
-    columns = Gather(column_slot, into_ref, mid, sems[7:], sent)
-    greet(heads.peers())
-    for p in range(PIECES):
-        heads.start(p)
-    rest = pltpu.make_async_copy(own_columns(x), rest_ref, rest_sem)
-    rest.start()
-    rest.wait()
-    rows = mid.shape[0] // PIECES
-    for step in range(2 * PIECES + 2):
-        for stage in range(3):
-            part = step - stage
-            if part < 0 or part >= 2 * PIECES:
-                continue
-            gather, p = (heads, part) if part < PIECES else (columns, part - PIECES)
-            if stage == 0:
-                gather.along_z(p)
-            elif stage == 1:
-                gather.along_y(p)
-            else:
-                gather.whole(p)
-                if gather is heads:
-                    project_piece(all_ref, wo_ref, 0, rest_ref, into_ref, p)
-                    columns.start(p)
-                else:
-                    span = pl.ds(p * rows, rows)
-                    project_rows(
-                        mid[span, :].astype(jnp.float32), gain_ref[1], lambda part: w_ref[1, part],
-                        (q_ref, k_ref, v_ref), span,
-                    )
-    attend_blocks(q_ref, k_ref, v_ref, flags, out_ref)
-    for wait in sent:
-        wait()
-
-
-def turn(own, x, wo, gains, w, flags):
-    dma = pltpu.SemaphoreType.DMA
-    vmem = pl.BlockSpec(memory_space=pltpu.VMEM)
-    rows, wide = x.shape
-    narrow = pltpu.VMEM((rows, HD), jnp.bfloat16)
-    return pl.pallas_call(
-        turn_kernel,
-        out_shape=(jax.ShapeDtypeStruct((rows, wide), x.dtype), jax.ShapeDtypeStruct((rows, HD), x.dtype)),
-        in_specs=[ANY, ANY, vmem, vmem, vmem, pl.BlockSpec(memory_space=pltpu.SMEM)],
-        out_specs=(vmem, vmem),
-        scratch_shapes=[pltpu.VMEM((rows, wide), jnp.bfloat16)] + [narrow] * 5 + [dma(())]
-        + gather_sems() + gather_sems(),
-        compiler_params=pltpu.CompilerParams(
-            collective_id=1, has_side_effects=True, vmem_limit_bytes=48 * 2**20
-        ),
-        name="turn",
-    )(own, x, wo, gains, w, flags)
-
-
-def spread_kernel(
-    feats, gain, w_qkv, w_out, xg, gains, wq, wo,
+def main_kernel(
+    feats, gain, w_qkv, w_out, flags, mid, out_ref, wo,
+    xg, gains, wq, all_ref, own, rest_ref, into_ref, q_ref, k_ref, v_ref,
     l_sem, x_send, x_recv, z_send, z_recv, y_send, y_recv, b_send, b_recv,
-    g_send, g_recv, q_send, q_recv, qx_send, qx_recv, o_send, o_recv,
+    g_send, g_recv, q_send, q_recv, qx_send, qx_recv, o_send, o_recv, rest_sem, *sems,
 ):
     core, x, y, z = place()
     node = z * 2 + x
@@ -355,17 +297,56 @@
         return wq.at[c, :, pl.ds(pl.multiple_of((zz * 2 + xx) * depth, depth), depth), :]
 
     own_rows = depth_rows(core, x, z)
+    weights = []
     for d in range(4):
         zz = z_apart(z, d)
         for other_core in range(2):
             target = 1 - core if other_core else core
             if d == 0 and not other_core:
                 keep(head_columns(z, core), own_rows, l_sem.at[2])
-                send(head_columns(z, core), own_rows, qx_send.at[0], qx_recv.at[0], across)
+                weights.append(remote(head_columns(z, core), own_rows, qx_send.at[0], qx_recv.at[0], across))
             else:
                 at = 2 * d + other_core
-                send(head_columns(zz, target), own_rows, q_send.at[at], q_recv.at[at], dev(target, x, y, zz))
-
+                weights.append(
+                    remote(head_columns(zz, target), own_rows, q_send.at[at], q_recv.at[at], dev(target, x, y, zz))
+                )
+
+    def start_weights():
+        for copy in weights:
+            copy.start()
+
+    def pass_section(s):
+        for d in range(4):
+            at = 2 * d + (core if s == 0 else 1 - core)
+            got = depth_rows(s, x, z_apart(z, d))
+            arrived = remote(head_columns(z, core), got, x_send, q_recv.at[at], sibling)
+            if d:
+                arrived.wait_recv()
+                send(got, got, qx_send.at[at], qx_recv.at[at], across)
+            else:
+                copy = remote(got, got, qx_send.at[1], qx_recv.at[1], across)
+
+                @pl.when(core != s)
+                def _():
+                    arrived.wait_recv()
+                    copy.start()
+
+                if s == 0:
+                    weights.append(copy)
+
+    def await_section(s):
+        for d in range(4):
+            at = 2 * d + (core if s == 0 else 1 - core)
+            got = depth_rows(s, 1 - x, z_apart(z, d))
+            remote(head_columns(z, core), got, x_send, qx_recv.at[at], sibling).wait_recv()
+
+    def await_projection():
+        for yy in range(2):
+            for cc in range(2):
+                got = wo.at[cc, pl.ds(yy * half_rows, half_rows), :]
+                remote(w_out.at[0, :, pl.ds(0, HD)], got, x_send, o_recv.at[2 * yy + cc], sibling).wait_recv()
+
+    pl.when(core == 0)(start_weights)
     for k in range(2):
         xx = 1 - x if k else x
         for d in (1, 2, 3):
@@ -373,6 +354,19 @@
             remote(mine, got, x_send, z_recv.at[3 * k + d - 1], sibling).wait_recv()
             send(got, got, y_send.at[4 * k + d], y_recv.at[4 * k + d], beside)
             send(got, got, b_send.at[8 * k + d], b_recv.at[8 * k + d], sibling)
+    pl.when(core == 1)(start_weights)
+    pass_section(0)
+    for k in range(2):
+        xx = 1 - x if k else x
+        for d in range(4):
+            got = region(core, xx, 1 - y, z_apart(z, d))
+            remote(mine, got, x_send, y_recv.at[4 * k + d], sibling).wait_recv()
+            send(got, got, b_send.at[8 * k + 4 + d], b_recv.at[8 * k + 4 + d], sibling)
+    for k in range(2):
+        xx = 1 - x if k else x
+        for d in range(8):
+            got = region(1 - core, xx, y if d < 4 else 1 - y, z_apart(z, d % 4))
+            remote(mine, got, x_send, b_recv.at[8 * k + d], sibling).wait_recv()
     half_rows = w_out.shape[1]
     to = wo.at[core, pl.ds(pl.multiple_of(y * half_rows, half_rows), half_rows), :]
     projections = []
@@ -390,63 +384,86 @@
                 copy.start()
             projections.append(copy)
 
-    for d in range(4):
-        for other_core in range(2):
-            at = 2 * d + other_core
-            if at == 0:
-                continue
-            got = depth_rows(1 - core if other_core else core, x, z_apart(z, d))
-            remote(head_columns(z, core), got, x_send, q_recv.at[at], sibling).wait_recv()
-            send(got, got, qx_send.at[at], qx_recv.at[at], across)
-    for k in range(2):
-        xx = 1 - x if k else x
-        for d in range(4):
-            got = region(core, xx, 1 - y, z_apart(z, d))
-            remote(mine, got, x_send, y_recv.at[4 * k + d], sibling).wait_recv()
-            send(got, got, b_send.at[8 * k + 4 + d], b_recv.at[8 * k + 4 + d], sibling)
-    for k in range(2):
-        xx = 1 - x if k else x
-        for d in range(8):
-            got = region(1 - core, xx, y if d < 4 else 1 - y, z_apart(z, d % 4))
-            remote(mine, got, x_send, b_recv.at[8 * k + d], sibling).wait_recv()
-    for d in range(4):
-        for other_core in range(2):
-            at = 2 * d + other_core
-            got = depth_rows(1 - core if other_core else core, 1 - x, z_apart(z, d))
-            remote(head_columns(z, core), got, x_send, qx_recv.at[at], sibling).wait_recv()
     remote(gain, gains.at[1 - core], g_send, g_recv, sibling).wait_recv()
-    for yy in range(2):
-        for cc in range(2):
-            got = wo.at[cc, pl.ds(yy * half_rows, half_rows), :]
-            remote(w_out.at[0, :, pl.ds(0, HD)], got, x_send, o_recv.at[2 * yy + cc], sibling).wait_recv()
-    for copy in sent:
-        copy.wait_send()
     for copy in local:
         copy.wait()
+    await_section(0)
+    rest = pltpu.make_async_copy(own_columns(xg), rest_ref, rest_sem)
+    rest.start()
+    for p in range(PIECES):
+        span = pl.ds(p * (xg.shape[0] // PIECES), xg.shape[0] // PIECES)
+        project_rows(
+            xg[span, :].astype(jnp.float32), gains[0], lambda part: wq[0, part], (q_ref, k_ref, v_ref), span
+        )
+    attend_blocks(q_ref, k_ref, v_ref, flags, own)
+    rest.wait()
+    waits = []
+    heads = Gather(head_slot, own, all_ref, sems[:7], waits)
+    columns = Gather(column_slot, into_ref, mid, sems[7:], waits)
+    for p in range(PIECES):
+        heads.start(p)
+    pass_section(1)
+    rows = mid.shape[0] // PIECES
+    for step in range(2 * PIECES + 2):
+        for stage in range(3):
+            part = step - stage
+            if part < 0 or part >= 2 * PIECES:
+                continue
+            gather, p = (heads, part) if part < PIECES else (columns, part - PIECES)
+            if stage == 0:
+                gather.along_z(p)
+            elif stage == 1:
+                gather.along_y(p)
+            else:
+                gather.whole(p)
+                if part == 0:
+                    await_projection()
+                if part == PIECES:
+                    await_section(1)
+                if gather is heads:
+                    project_piece(all_ref, wo, 0, rest_ref, into_ref, p)
+                    columns.start(p)
+                else:
+                    span = pl.ds(p * rows, rows)
+                    project_rows(
+                        mid[span, :].astype(jnp.float32), gains[1], lambda part: wq[1, part],
+                        (q_ref, k_ref, v_ref), span,
+                    )
+    attend_blocks(q_ref, k_ref, v_ref, flags, out_ref)
+    for copy in sent + weights:
+        copy.wait_send()
     pl.when(x != y)(projections[0].wait_send)
     for copy in projections[1:]:
         copy.wait_send()
-
-
-def spread(feats, gain, w_qkv, w_out):
+    for wait in waits:
+        wait()
+
+
+def first_layer(feats, gain, w_qkv, w_out, flags):
     dma = pltpu.SemaphoreType.DMA
+    vmem = pl.BlockSpec(memory_space=pltpu.VMEM)
     bf = jnp.bfloat16
     rows, wide = feats.shape[1] * 8, feats.shape[2] * 2
+    narrow = pltpu.VMEM((rows, HD), bf)
     return pl.pallas_call(
-        spread_kernel,
+        main_kernel,
         out_shape=(
             jax.ShapeDtypeStruct((rows, wide), bf),
-            jax.ShapeDtypeStruct((2, 1, wide), jnp.float32),
-            jax.ShapeDtypeStruct((2, 3, wide, HD), bf),
+            jax.ShapeDtypeStruct((rows, HD), bf),
             jax.ShapeDtypeStruct((2, wide, HD), bf),
         ),
-        in_specs=[ANY] * 4,
-        out_specs=(ANY,) * 4,
-        scratch_shapes=[dma((3,)), dma(()), dma(()), dma((6,)), dma((6,)), dma((8,)), dma((8,)), dma((16,)), dma((16,)),
-                        dma(()), dma(()), dma((8,)), dma((8,)), dma((8,)), dma((8,)), dma((4,)), dma((4,))],
-        compiler_params=pltpu.CompilerParams(collective_id=0, has_side_effects=True),
-        name="spread",
-    )(feats, gain, w_qkv, w_out)
+        in_specs=[ANY] * 4 + [pl.BlockSpec(memory_space=pltpu.SMEM)],
+        out_specs=(vmem,) * 3,
+        scratch_shapes=[pltpu.VMEM((rows, wide), bf), pltpu.VMEM((2, 1, wide), jnp.float32),
+                        pltpu.VMEM((2, 3, wide, HD), bf), pltpu.VMEM((rows, wide), bf)] + [narrow] * 6
+        + [dma((3,)), dma(()), dma(()), dma((6,)), dma((6,)), dma((8,)), dma((8,)), dma((16,)), dma((16,)),
+           dma(()), dma(()), dma((8,)), dma((8,)), dma((8,)), dma((8,)), dma((4,)), dma((4,)), dma(())]
+        + gather_sems() + gather_sems(),
+        compiler_params=pltpu.CompilerParams(
+            collective_id=0, has_side_effects=True, vmem_limit_bytes=48 * 2**20
+        ),
+        name="first_layer",
+    )(feats, gain, w_qkv, w_out, flags)
 
 
 def finish_kernel(
@@ -600,44 +617,10 @@
         out_ref[span, :] = (summed / total).astype(jnp.bfloat16)
 
 
-def attend_kernel(x_ref, gain_ref, w_ref, flags, out_ref, q_ref, k_ref, v_ref):
-    step = x_ref.shape[0]
-    at = pl.program_id(0)
-    here = pl.ds(pl.multiple_of(at * step, step), step)
-    project_rows(
-        x_ref[...].astype(jnp.float32), gain_ref[0], lambda part: w_ref[0, part], (q_ref, k_ref, v_ref), here
-    )
-
-    @pl.when(at == pl.num_programs(0) - 1)
-    def _():
-        attend_blocks(q_ref, k_ref, v_ref, flags, out_ref)
-
-
-def attend(x, gains, w, flags, s):
-    rows, wide = x.shape
-    step = rows // 4
-    return pl.pallas_call(
-        attend_kernel,
-        grid=(4,),
-        out_shape=jax.ShapeDtypeStruct((rows, HD), jnp.bfloat16),
-        in_specs=[
-            pl.BlockSpec((step, wide), lambda i: (i, 0)),
-            pl.BlockSpec((1, 1, wide), lambda i: (s, 0, 0)),
-            pl.BlockSpec((1, 3, wide, HD), lambda i: (s, 0, 0, 0)),
-            pl.BlockSpec(memory_space=pltpu.SMEM),
-        ],
-        out_specs=pl.BlockSpec((rows, HD), lambda i: (0, 0)),
-        scratch_shapes=[pltpu.VMEM((rows, HD), jnp.bfloat16)] * 3,
-        compiler_params=pltpu.CompilerParams(vmem_limit_bytes=40 * 2**20),
-        name="attend",
-    )(x, gains, w, flags)
-
-
 def local_planes(feats, gain, w_qkv, w_out, block_mask):
     core, micro, y, z = place()
     flags = lax.dynamic_index_in_dim(block_mask, micro, 0, keepdims=False)
-    whole, gains, wq, wo = spread(feats, gain, w_qkv, w_out)
-    mid, attended = turn(attend(whole, gains, wq, flags, 0), whole, wo, gains, wq, flags)
+    mid, attended, wo = first_layer(feats, gain, w_qkv, w_out, flags)
     return finish_layers(attended, mid, wo)[None]
 
 

time: 194 us -> 183 us (0.943)
  Pallas kernels: 185 us -> 174 us
    pallas_call x3 -> x1, Pallas kernels: 141 us -> 130 us  [first_layer(): pl.pallas_call(main_kernel, out_shape=(jax.ShapeDtypeStruct((rows, wide),...]
    unnamed x17 -> x13, local copies, waits for them, and re-layouts: 8.47 us -> 7.86 us
where the time goes in v4:
time: 183 us; the launch traced here: 182 us
  Pallas kernels  174 us (95%)
  local copies, waits for them, and re-layouts  7.86 us (4%)
    pallas_call x1, Pallas kernels, first_layer(): pl.pallas_call(main_kernel, out_shape=(jax.ShapeDtypeStruct((rows, wide),...  130 us
    pallas_call x1, Pallas kernels, finish_layers(): pl.pallas_call(finish_kernel, out_shape=jax.ShapeDtypeStruct((2, rows //...  45 us
    unnamed x13, local copies, waits for them, and re-layouts  7.86 us

profile of v4, /device:TPU:25, one launch (start us, length us, event | category | flops | bytes accessed | tf_op | source)
XLA Modules:
  0.0 182.4 jit_solution(1654248620646506116)
XLA Ops:
  0.0 0.0 copy-start
  0.0 0.7 copy-done
  0.7 0.0 copy-start.2
  0.7 1.4 copy-done.2
  2.1 0.0 copy-start.3
  2.1 1.0 copy-done.3
  3.2 0.0 copy-start.4
  3.2 1.0 copy-done.4
  4.2 0.0 copy-start.5
  4.2 0.7 copy-done.5
  4.9 129.5 %first_layer.1 = (bf16[1024,2048]{1,0:T(8,128)(2,1)}, bf16[1024,128]{1,0:T(8,128)(2,1)S(1)}, bf16[2,2048,128]{2,1,0:T(8,128)(2,1)S(1)}) custom-call(bf16[2,128,1024]{2,1,0:T(8,128)(2,1)S(1)} %copy-done.3, f32[1,2048]{1,0:T(1,128)S(1)} %copy-done.5, bf16[1,3,256,1024]{3,2,1,0:T(8,128)(2,1)S(1)} %copy-done.2, bf16[1,1024,256]{2,1,0:T(8,128)(2,1)S(1)} %copy-done.4, ...), custom_call_target="tpu_custom_call" | custom-call | tf_op jit(solution)/shard_map/first_layer/pallas_call | solution.py:448
  134.4 0.0 copy-start.1
  134.5 2.2 %copy-done.1 = bf16[1024,2048]{1,0:T(8,128)(2,1)S(1)} copy-done((bf16[1024,2048]{1,0:T(8,128)(2,1)S(1)}, bf16[1024,2048]{1,0:T(8,128)(2,1)}, u32[]{:S(2)}) %copy-start.1) | copy-done | bytes 4194328
  136.6 45.0 %finish.1 = bf16[2,128,1024]{2,1,0:T(8,128)(2,1)S(1)} custom-call(bf16[1024,128]{1,0:T(8,128)(2,1)S(1)} %get-tuple-element.8.own, bf16[1024,2048]{1,0:T(8,128)(2,1)S(1)} %copy-done.1, bf16[2,2048,128]{2,1,0:T(8,128)(2,1)S(1)} %get-tuple-element.10.wo_ref), custom_call_target="tpu_custom_call" | custom-call | tf_op jit(solution)/shard_map/finish/pallas_call | solution.py:572
  181.6 0.8 copy.7
  (1 shorter events, 0.0 us)
Async XLA Ops:
  0.0 0.7 copy-start
  0.7 1.4 copy-start.2
  2.1 1.0 copy-start.3
  3.2 1.0 copy-start.4
  4.2 0.7 copy-start.5
  134.4 2.2 %copy-start.1 = (bf16[1024,2048]{1,0:T(8,128)(2,1)S(1)}, bf16[1024,2048]{1,0:T(8,128)(2,1)}, u32[]{:S(2)}) copy-start(bf16[1024,2048]{1,0:T(8,128)(2,1)} %get-tuple-element.9.mid) | copy-start | bytes 12582916

commit v5 on v4

--- a/solution.py
+++ b/solution.py
@@ -460,7 +460,7 @@
            dma(()), dma(()), dma((8,)), dma((8,)), dma((8,)), dma((8,)), dma((4,)), dma((4,)), dma(())]
         + gather_sems() + gather_sems(),
         compiler_params=pltpu.CompilerParams(
-            collective_id=0, has_side_effects=True, vmem_limit_bytes=48 * 2**20
+            collective_id=0, has_side_effects=True, vmem_limit_bytes=63 * 2**20
         ),
         name="first_layer",
     )(feats, gain, w_qkv, w_out, flags)
@@ -577,7 +577,7 @@
         scratch_shapes=[pltpu.VMEM((rows, wide), jnp.bfloat16), narrow, narrow]
         + [dma(()), dma(()), dma(()), dma(()), dma((8,)), dma((16,))] + gather_sems(),
         compiler_params=pltpu.CompilerParams(
-            collective_id=3, has_side_effects=True, vmem_limit_bytes=40 * 2**20
+            collective_id=3, has_side_effects=True, vmem_limit_bytes=63 * 2**20
         ),
         name="finish",
     )(own, mid, wo)

time: 183 us -> 180 us (0.984)
  local copies, waits for them, and re-layouts: 7.86 us -> 3.16 us
  Pallas kernels: 174 us -> 177 us
    unnamed x13 -> x3, local copies, waits for them, and re-layouts: 7.86 us -> 2.57 us
where the time goes in v5:
time: 180 us
  Pallas kernels  177 us (98%)
  local copies, waits for them, and re-layouts  3.16 us (2%)
    pallas_call x1, Pallas kernels, first_layer(): pl.pallas_call(main_kernel, out_shape=(jax.ShapeDtypeStruct((rows, wide),...  131 us
    pallas_call x1, Pallas kernels, finish_layers(): pl.pallas_call(finish_kernel, out_shape=jax.ShapeDtypeStruct((2, rows //...  45.8 us

profile of v5, /device:TPU:25, one launch (start us, length us, event | category | flops | bytes accessed | tf_op | source)
XLA Modules:
  0.0 180.2 jit_solution(3305561126659660808)
XLA Ops:
  0.0 0.0 copy-start
  0.0 0.7 copy-done
  0.7 0.6 dynamic-slice_bitcast_fusion.flags
  1.3 131.2 %first_layer.1 = (bf16[1024,2048]{1,0:T(8,128)(2,1)}, bf16[1024,128]{1,0:T(8,128)(2,1)}, bf16[2,2048,128]{2,1,0:T(8,128)(2,1)}) custom-call(bf16[2,128,1024]{2,1,0:T(8,128)(2,1)} %feats.1, f32[1,2048]{1,0:T(1,128)} %gain.1, bf16[1,3,256,1024]{3,2,1,0:T(8,128)(2,1)} %w_qkv.1, bf16[1,1024,256]{2,1,0:T(8,128)(2,1)} %w_out.1, s32[8,8]{1,0:T(8,128)} %dynamic-slice_bitcast_fusion.flags), custom_call_target="tpu_custom_call" | custom-call | tf_op jit(solution)/shard_map/first_layer/pallas_call | solution.py:448
  132.5 45.8 %finish.1 = bf16[2,128,1024]{2,1,0:T(8,128)(2,1)} custom-call(bf16[1024,128]{1,0:T(8,128)(2,1)} %get-tuple-element.8.own, bf16[1024,2048]{1,0:T(8,128)(2,1)} %get-tuple-element.9.mid, bf16[2,2048,128]{2,1,0:T(8,128)(2,1)} %get-tuple-element.10.wo_ref), custom_call_target="tpu_custom_call" | custom-call | tf_op jit(solution)/shard_map/finish/pallas_call | solution.py:572
  178.3 1.9 %copy.7 = bf16[1,2,128,1024]{3,2,1,0:T(8,128)(2,1)} copy(bf16[1,2,128,1024]{3,2,1,0:T(8,128)(2,1)} %bitcast.3) | data formatting | bytes 1048576
Async XLA Ops:
  0.0 0.7 copy-start
